TPU v7x, 32 devices: a whole 2x2x4 slice. The times are simulated.
32 devices in a mesh: seq: 4 (over y, x), fsdp: 8 (over z, core).
Axes of the slice: x: 2, y: 2, z: 4, core: 2. Of those that a mesh axis runs over, the one named last changes fastest.
Arguments:
- inputs: bfloat16 [8, 1024, 2048], P('fsdp', 'seq'), may hold values from -40 to 40
- cotangent: bfloat16 [8, 1024, 2048], P('fsdp', 'seq'), may hold values from -6 to 6
- segments: int32 [8, 1024], P('fsdp'), may hold values from 0 to 7, never falling along the last dimension, each value on 1 to 256 neighbouring positions
- valid: int32 [8, 1024], P('fsdp', 'seq'), may hold values from 0 to 1, as said below
- norm_attn: bfloat16 [2048], P('fsdp'), may hold values from 0.5 to 1.5
- query_weight: bfloat16 [2048, 2048], P('fsdp'), may hold values from -0.0625 to 0.0625
- w_key: bfloat16 [2048, 2048], P('fsdp'), may hold values from -0.0625 to 0.0625
- w_value: bfloat16 [2048, 2048], P('fsdp'), may hold values from -0.125 to 0.125
- w_out: bfloat16 [2048, 2048], P('fsdp'), may hold values from -0.5 to 0.5
- rel_bias: bfloat16 [32, 32], replicated, may hold values from -4 to 4
- norm_ff: bfloat16 [2048], P('fsdp'), may hold values from 0.5 to 1.5
- w_gate: bfloat16 [2048, 5120], P('fsdp'), may hold values from -0.125 to 0.125
- w_up: bfloat16 [2048, 5120], P('fsdp'), may hold values from -0.125 to 0.125
- w_down: bfloat16 [2048, 5120], P('fsdp'), may hold values from -0.078125 to 0.078125
Outputs:
- output: bfloat16 [8, 1024, 2048], P('fsdp', 'seq')
- grad_inputs: bfloat16 [8, 1024, 2048], P('fsdp', 'seq')
- grad_norm_attn: float32 [2048], P('fsdp')
- grad_query: float32 [2048, 2048], P('fsdp')
- grad_key: float32 [2048, 2048], P('fsdp')
- grad_value: float32 [2048, 2048], P('fsdp')
- grad_out: float32 [2048, 2048], P('fsdp')
- grad_rel_bias: float32 [32, 32], replicated
- grad_norm_ff: float32 [2048], P('fsdp')
- grad_gate: float32 [2048, 5120], P('fsdp')
- grad_up: float32 [2048, 5120], P('fsdp')
- grad_down: float32 [2048, 5120], P('fsdp')
- rms_stats: float32 [4], replicated
Inputs may be any that keep to these rules, and one draw needn't show every extreme that they name: `segments`: segment numbers never fall along a sequence; a document has 1 to 256 tokens, and some document of each sequence has exactly that many. In each sequence the valid tokens are a prefix; the prefixes of the 8 sequences have the lengths 1024 // 4**k, k = 0 to 7, in some order.
All inputs are finite; a program needn't handle non-finite values.
Results may differ from a plain program's by a relative error of at most 0.02.
Values may be sent and summed in bfloat16 or wider, within the bound.
No kernel may reach another device: no remote copies, remote signals or barrier semaphores. Data moves between devices by JAX's collectives and lax.ppermute only.
A program may use at most 384 MiB of HBM per device.

v0:
```python
import jax
import jax.numpy as jnp
from jax import lax
from jax.sharding import PartitionSpec as P

DH = 64


epsilon = 1e-06
masked_score = -1e30
far_steps = (12, 16, 23, 32, 46, 64, 91)


def bucket_of(relative):
    distance = jnp.abs(relative)
    far_bucket = jnp.full(relative.shape, 8, jnp.int32)
    for threshold in far_steps:
        far_bucket = far_bucket + (distance >= threshold).astype(jnp.int32)
    near_bucket = jnp.where(distance < 8, distance, far_bucket)
    return near_bucket + 16 * (relative > 0).astype(jnp.int32)


def onehot_piece(offset, sub_rows, length, buckets):
    query_pos = offset + jnp.arange(sub_rows, dtype=jnp.int32)
    key_pos = jnp.arange(length, dtype=jnp.int32)
    labels = bucket_of(key_pos[None, :] - query_pos[:, None])
    return (labels[None, :, :] == jnp.arange(buckets, dtype=jnp.int32)[:, None, None]).astype(
        jnp.bfloat16
    )


def block_bias(partial_bias_table, first_row, row_count, length):
    buckets, head_count = partial_bias_table.shape
    sub_rows = min(128, row_count)

    def block_add_piece(step_index, filled):
        offset = step_index * sub_rows
        bucket_indicator = onehot_piece(first_row + offset, sub_rows, length, buckets)
        part_bias = jnp.einsum(
            "ftn,fm->mtn", bucket_indicator, partial_bias_table, preferred_element_type=jnp.float32
        )
        return lax.dynamic_update_slice_in_dim(filled, part_bias, offset, 1)

    return lax.fori_loop(
        0,
        row_count // sub_rows,
        block_add_piece,
        jnp.zeros((head_count, row_count, length), jnp.float32),
    )


def bias_grad(d_scores, first_row, buckets):
    head_count, row_count, length = d_scores.shape
    sub_rows = min(128, row_count)

    def bias_add_piece(step_index, running):
        offset = step_index * sub_rows
        partial_score_rows = lax.dynamic_slice_in_dim(d_scores, offset, sub_rows, 1)
        bucket_indicator = onehot_piece(first_row + offset, sub_rows, length, buckets)
        return running + jnp.einsum(
            "vrp,nrp->nv", partial_score_rows, bucket_indicator, preferred_element_type=jnp.float32
        )

    return lax.fori_loop(
        0, row_count // sub_rows, bias_add_piece, jnp.zeros((buckets, head_count), jnp.float32)
    )


def scores_of(block_query, key_rows, partial_bias_table, seg_row, first_row):
    row_count = block_query.shape[0]
    length = key_rows.shape[0]
    raw_scores = jnp.einsum(
        "qhd,khd->hqk", block_query, key_rows, preferred_element_type=jnp.float32
    )
    raw_scores = raw_scores + block_bias(partial_bias_table, first_row, row_count, length)
    same_doc = lax.dynamic_slice_in_dim(seg_row, first_row, row_count)[:, None] == seg_row[None, :]
    return jnp.where(same_doc[None, :, :], raw_scores, masked_score)


def gated_gelu(gate, up_proj):
    return jax.nn.gelu(gate, approximate=True) * up_proj


def on_device(
    inputs,
    cotangent,
    segments,
    valid,
    norm_attn,
    query_weight,
    w_key,
    w_value,
    w_out,
    rel_bias,
    norm_ff,
    w_gate,
    w_up,
    w_down,
):
    seq_index = lax.axis_index("seq")
    shard_index = lax.axis_index("fsdp")
    shard_rows = query_weight.shape[0]
    model_width = inputs.shape[2]
    hidden_units = w_gate.shape[1]
    x_in = inputs[0].astype(jnp.float32)
    grad_low = cotangent[0]
    grad_wide = grad_low.astype(jnp.float32)
    seg_row = segments[0]
    live_rows = valid[0].astype(jnp.float32)
    scale_one = lax.rsqrt(jnp.mean(x_in * x_in, axis=-1, keepdims=True) + epsilon)
    gain_piece = lax.all_gather(norm_attn, "fsdp", axis=0, tiled=True)
    query_piece = lax.all_gather(query_weight, "fsdp", axis=0, tiled=True)
    key_piece = lax.all_gather(w_key, "fsdp", axis=0, tiled=True)
    value_piece = lax.all_gather(w_value, "fsdp", axis=0, tiled=True)
    out_piece = lax.all_gather(w_out, "fsdp", axis=0, tiled=True)
    gain_wide = gain_piece.astype(jnp.float32)
    normed = (x_in * scale_one * gain_wide[None, :]).astype(jnp.bfloat16)
    gain_one = gain_wide
    acc_query = jnp.dot(normed, query_piece, preferred_element_type=jnp.float32)
    acc_key = jnp.dot(normed, key_piece, preferred_element_type=jnp.float32)
    acc_value = jnp.dot(normed, value_piece, preferred_element_type=jnp.float32)
    queries = acc_query.astype(jnp.bfloat16)
    key_proj = acc_key.astype(jnp.bfloat16)
    value_proj = acc_value.astype(jnp.bfloat16)
    head_query, head_key, head_value = (
        lax.all_to_all(queries, "seq", split_axis=1, concat_axis=0, tiled=True),
        lax.all_to_all(key_proj, "seq", split_axis=1, concat_axis=0, tiled=True),
        lax.all_to_all(value_proj, "seq", split_axis=1, concat_axis=0, tiled=True),
    )
    seq_len = head_query.shape[0]
    local_width = head_query.shape[1]
    heads_local = local_width // DH
    head_shape = (seq_len, heads_local, DH)
    query_three = head_query.reshape(head_shape)
    key_three = head_key.reshape(head_shape)
    value_three = head_value.reshape(head_shape)
    partial_bias_table = lax.dynamic_slice_in_dim(rel_bias, seq_index * heads_local, heads_local, 1)
    bucket_total = rel_bias.shape[0]
    block_rows = min(512, seq_len)
    block_count = seq_len // block_rows
    block_starts = block_rows * jnp.arange(block_count, dtype=jnp.int32)
    query_blocks = query_three.reshape(block_count, block_rows, heads_local, DH)

    def forward_block(element):
        block_query, first_row = element
        scores = scores_of(block_query, key_three, partial_bias_table, seg_row, first_row)
        top_score = jnp.max(scores, axis=-1, keepdims=True)
        expo_scores = jnp.exp(scores - top_score)
        row_total = jnp.sum(expo_scores, axis=-1, keepdims=True)
        weights = (expo_scores / row_total).astype(jnp.bfloat16)
        block_out = jnp.einsum(
            "hqk,khd->qhd", weights, value_three, preferred_element_type=jnp.float32
        )
        return (block_out.astype(jnp.bfloat16), (top_score + jnp.log(row_total))[:, :, 0])

    head_out, block_logs = lax.map(forward_block, (query_blocks, block_starts))
    context = lax.all_to_all(
        head_out.reshape(seq_len, local_width), "seq", split_axis=0, concat_axis=1, tiled=True
    )
    attn_out = jnp.einsum("tc,oc->to", context, out_piece, preferred_element_type=jnp.float32)
    middle = x_in + attn_out
    scale_two = lax.rsqrt(jnp.mean(middle * middle, axis=-1, keepdims=True) + epsilon)
    gain_piece = lax.all_gather(norm_ff, "fsdp", axis=0, tiled=True)
    gate_piece = lax.all_gather(w_gate, "fsdp", axis=0, tiled=True)
    up_piece = lax.all_gather(w_up, "fsdp", axis=0, tiled=True)
    gain_wide = gain_piece.astype(jnp.float32)
    normed = (middle * scale_two * gain_wide[None, :]).astype(jnp.bfloat16)
    gate = jnp.dot(normed, gate_piece, preferred_element_type=jnp.float32)
    up_proj = jnp.dot(normed, up_piece, preferred_element_type=jnp.float32)
    hidden_wide, act_back = jax.vjp(gated_gelu, gate, up_proj)
    hidden = hidden_wide.astype(jnp.bfloat16)
    ff_out = jnp.einsum(
        "tf,of->to",
        hidden,
        lax.all_gather(w_down, "fsdp", axis=0, tiled=True),
        preferred_element_type=jnp.float32,
    )
    output = (middle + ff_out).astype(jnp.bfloat16)[None]

    def live_sum(value_vectors):
        return jnp.sum(live_rows * jnp.sum(value_vectors * value_vectors, axis=-1))

    square_sums = jnp.stack(
        [live_sum(x_in), live_sum(attn_out), live_sum(middle), live_sum(ff_out)]
    )
    live_count = jnp.sum(live_rows)
    grad_cols = grad_low
    d_hidden = jnp.dot(
        grad_cols,
        lax.all_gather(w_down, "fsdp", axis=0, tiled=True),
        preferred_element_type=jnp.float32,
    )
    d_gate_wide, d_up_wide = act_back(d_hidden)
    d_gate = d_gate_wide.astype(jnp.bfloat16)
    d_up = d_up_wide.astype(jnp.bfloat16)
    pieces = lax.all_gather((w_gate, w_up), "fsdp", axis=0, tiled=True)
    d_normed_two = jnp.einsum(
        "tf,of->to", d_gate, pieces[0], preferred_element_type=jnp.float32
    ) + jnp.einsum("tf,of->to", d_up, pieces[1], preferred_element_type=jnp.float32)
    second_unit_gradient = d_normed_two * gain_wide[None, :]
    grad_gain_two = jnp.sum(d_normed_two * (middle * scale_two), axis=0)
    d_middle = (
        grad_wide
        + scale_two * second_unit_gradient
        - middle * scale_two**3 * jnp.mean(second_unit_gradient * middle, axis=-1, keepdims=True)
    )
    d_attn = d_middle.astype(jnp.bfloat16)
    d_context_wide = jnp.dot(d_attn, out_piece, preferred_element_type=jnp.float32)
    d_context = d_context_wide.astype(jnp.bfloat16)
    d_head_out = lax.all_to_all(d_context, "seq", split_axis=1, concat_axis=0, tiled=True)
    dout_blocks = d_head_out.reshape(block_count, block_rows, heads_local, DH)

    def backward_block(running, element):
        d_key_acc, d_value_acc, d_table = running
        block_query, block_dout, block_log, first_row = element
        scores = scores_of(block_query, key_three, partial_bias_table, seg_row, first_row)
        prob_exact = jnp.exp(scores - block_log[:, :, None])
        d_probs = jnp.einsum(
            "qhd,khd->hqk", block_dout, value_three, preferred_element_type=jnp.float32
        )
        row_dot = jnp.sum(prob_exact * d_probs, axis=-1, keepdims=True)
        d_scores = (prob_exact * (d_probs - row_dot)).astype(jnp.bfloat16)
        d_query_block = jnp.einsum(
            "hqk,khd->qhd", d_scores, key_three, preferred_element_type=jnp.float32
        )
        d_key_acc = d_key_acc + jnp.einsum(
            "hqk,qhd->khd", d_scores, block_query, preferred_element_type=jnp.float32
        )
        d_value_acc = d_value_acc + jnp.einsum(
            "hqk,qhd->khd",
            prob_exact.astype(jnp.bfloat16),
            block_dout,
            preferred_element_type=jnp.float32,
        )
        d_table = d_table + bias_grad(d_scores, first_row, bucket_total)
        return ((d_key_acc, d_value_acc, d_table), d_query_block.astype(jnp.bfloat16))

    empty_heads = jnp.zeros(head_shape, jnp.float32)
    (d_key_acc, d_value_acc, d_table), d_query_blocks = lax.scan(
        backward_block,
        (empty_heads, empty_heads, jnp.zeros((bucket_total, heads_local), jnp.float32)),
        (query_blocks, dout_blocks, block_logs, block_starts),
    )
    d_query_heads = d_query_blocks.reshape(seq_len, local_width)
    d_key_heads = d_key_acc.reshape(seq_len, local_width).astype(jnp.bfloat16)
    d_value_heads = d_value_acc.reshape(seq_len, local_width).astype(jnp.bfloat16)
    d_queries, d_keys, d_values = (
        lax.all_to_all(d_query_heads, "seq", split_axis=0, concat_axis=1, tiled=True),
        lax.all_to_all(d_key_heads, "seq", split_axis=0, concat_axis=1, tiled=True),
        lax.all_to_all(d_value_heads, "seq", split_axis=0, concat_axis=1, tiled=True),
    )
    pieces = lax.all_gather((query_weight, w_key, w_value), "fsdp", axis=0, tiled=True)
    d_normed_one = (
        jnp.einsum("te,de->td", d_queries, pieces[0], preferred_element_type=jnp.float32)
        + jnp.einsum("te,de->td", d_keys, pieces[1], preferred_element_type=jnp.float32)
        + jnp.einsum("te,de->td", d_values, pieces[2], preferred_element_type=jnp.float32)
    )
    d_unit_one = d_normed_one * gain_one[None, :]
    grad_gain_one = jnp.sum(d_normed_one * (x_in * scale_one), axis=0)
    d_input = (
        d_middle
        + scale_one * d_unit_one
        - x_in * scale_one**3 * jnp.mean(d_unit_one * x_in, axis=-1, keepdims=True)
    )
    grad_inputs = d_input.astype(jnp.bfloat16)[None]

    def trans_dot(left_side, right_side):
        return lax.dot_general(
            left_side, right_side, (((0,), (0,)), ((), ())), preferred_element_type=jnp.float32
        )

    normed_one = (x_in * scale_one * gain_one[None, :]).astype(jnp.bfloat16)
    normed_two = (middle * scale_two * gain_wide[None, :]).astype(jnp.bfloat16)
    grad_cols = grad_low
    summed_rows = lax.psum_scatter(
        jnp.concatenate(
            [
                trans_dot(normed_one, d_queries),
                trans_dot(normed_one, d_keys),
                trans_dot(normed_one, d_values),
                trans_dot(d_attn, context),
                trans_dot(normed_two, d_gate),
                trans_dot(normed_two, d_up),
                trans_dot(grad_cols, hidden),
            ],
            axis=1,
        ).astype(jnp.bfloat16),
        "fsdp",
        scatter_dimension=0,
        tiled=True,
    ).astype(jnp.float32)
    summed_rows = lax.psum(summed_rows.astype(jnp.bfloat16), "seq").astype(jnp.float32)
    grad_query = summed_rows[:, 0:model_width]
    grad_key = summed_rows[:, model_width : 2 * model_width]
    grad_value = summed_rows[:, 2 * model_width : 3 * model_width]
    grad_out = summed_rows[:, 3 * model_width : 4 * model_width]
    edge_two = 4 * model_width
    grad_gate = summed_rows[:, edge_two : edge_two + hidden_units]
    grad_up = summed_rows[:, edge_two + hidden_units : edge_two + 2 * hidden_units]
    grad_down = summed_rows[:, edge_two + 2 * hidden_units : edge_two + 3 * hidden_units]
    table_full = lax.dynamic_update_slice_in_dim(
        jnp.zeros(rel_bias.shape, jnp.float32), d_table, seq_index * heads_local, 1
    )
    gain_one_sum, gain_two_sum, table_sum, square_total, count_total = lax.psum(
        (grad_gain_one, grad_gain_two, table_full, square_sums, live_count), ("seq", "fsdp")
    )
    rms_stats = jnp.sqrt(square_total / (count_total * model_width))
    grad_norm_attn = lax.dynamic_slice_in_dim(gain_one_sum, shard_index * shard_rows, shard_rows)
    grad_norm_ff = lax.dynamic_slice_in_dim(gain_two_sum, shard_index * shard_rows, shard_rows)
    return (
        output,
        grad_inputs,
        grad_norm_attn,
        grad_query,
        grad_key,
        grad_value,
        grad_out,
        table_sum,
        grad_norm_ff,
        grad_gate,
        grad_up,
        grad_down,
        rms_stats,
    )


def solution(mesh):
    placed = (
        P("fsdp", "seq", None),
        P("fsdp", "seq", None),
        P("fsdp", None),
        P("fsdp", "seq"),
        P("fsdp"),
        P("fsdp", None),
        P("fsdp", None),
        P("fsdp", None),
        P("fsdp", None),
        P(),
        P("fsdp"),
        P("fsdp", None),
        P("fsdp", None),
        P("fsdp", None),
    )
    return jax.shard_map(
        on_device,
        mesh=mesh,
        in_specs=placed,
        out_specs=(
            P("fsdp", "seq", None),
            P("fsdp", "seq", None),
            P("fsdp"),
            P("fsdp", None),
            P("fsdp", None),
            P("fsdp", None),
            P("fsdp", None),
            P(),
            P("fsdp"),
            P("fsdp", None),
            P("fsdp", None),
            P("fsdp", None),
            P(),
        ),
        check_vma=False,
    )
```

profile of v0, /device:TPU:8, one launch (start us, length us, event | category | flops | bytes accessed | tf_op | source)
XLA Modules:
  0.0 2643.9 jit_solution(13975746930475007470)
XLA Ops:
  21.4 68.8 %all-gather.10.cloned.1.call-done = bf16[2048,2048]{1,0:T(8,128)(2,1)} async-done(((bf16[256,2048]{1,0:T(8,128)(2,1)}), bf16[2048,2048]{1,0:T(8,128)(2,1)}) %all-gather.10.cloned.1.call-update) | async-done | bytes 8388624 | tf_op jit(solution)/shard_map/all_gather | solution.py:112
  101.1 71.2 %all-gather.12.cloned.1.call-done = bf16[2048,2048]{1,0:T(8,128)(2,1)} async-done(((bf16[256,2048]{1,0:T(8,128)(2,1)}), bf16[2048,2048]{1,0:T(8,128)(2,1)}) %all-gather.12.cloned.1.call-update) | async-done | bytes 8388624 | tf_op jit(solution)/shard_map/all_gather | solution.py:113
  183.0 71.5 %all-gather.14.cloned.1.call-done = bf16[2048,2048]{1,0:T(8,128)(2,1)} async-done(((bf16[256,2048]{1,0:T(8,128)(2,1)}), bf16[2048,2048]{1,0:T(8,128)(2,1)}) %all-gather.14.cloned.1.call-update) | async-done | bytes 8388624 | tf_op jit(solution)/shard_map/all_gather | solution.py:114
  285.3 146.9 %while.72 = (s32[]{:T(128)}, bf16[2,512,8,64]{1,3,2,0:T(8,128)(2,1)}, f32[2,8,512]{2,1,0:T(8,128)}, s32[2]{0:T(128)}, s32[1024]{0:T(1024)S(1)}, /*index=5*/s32[1...) while((s32[]{:T(128)}, ...), condition=%wide.region_6.7_spmd, body=%wide.region_1.6_spmd.sunk | while | flops 1183051904 | bytes 177352736 | solution.py:156
  294.7 32.9 %while.76 = (s32[]{:T(128)}, f32[8,512,1024]{2,1,0:T(8,128)}, s32[]{:T(128)}, bf16[32,8]{0,1:T(8,128)(2,1)S(1)}, s32[]{:T(128)}, /*index=5*/s32[]{:T(128)}, s32[]{:T(128)}, s32[]{:T(128)}) while((s32[]{:T(128)}, f32[8,512,1024]{2,1,0:T(8,128)}, s32[]{:T(128)}, bf16[32,8]{0,1:T(8,128)(2,1)S(1)}, s32[]{:T(128)}, /*index=5*/s32[]{:T(128)}, ...), condition=%wide.region_3.3_spmd, body=%wide.region_2.2_spmd.sunk | while | flops 74973320 | bytes 13633183 | solution.py:44
  369.4 32.9 %while.76 = (s32[]{:T(128)}, f32[8,512,1024]{2,1,0:T(8,128)}, s32[]{:T(128)}, bf16[32,8]{0,1:T(8,128)(2,1)S(1)}, s32[]{:T(128)}, /*index=5*/s32[]{:T(128)}, s32[]{:T(128)}, s32[]{:T(128)}) while((s32[]{:T(128)}, f32[8,512,1024]{2,1,0:T(8,128)}, s32[]{:T(128)}, bf16[32,8]{0,1:T(8,128)(2,1)S(1)}, s32[]{:T(128)}, /*index=5*/s32[]{:T(128)}, ...), condition=%wide.region_3.3_spmd, body=%wide.region_2.2_spmd.sunk | while | flops 74973320 | bytes 13633183 | solution.py:44
  436.3 14.3 all_to_all.109
  457.2 12.4 all-gather.1
  479.0 42.7 %all-gather.18.cloned.1.call-done = bf16[2048,5120]{1,0:T(8,128)(2,1)} async-done(((bf16[256,5120]{1,0:T(8,128)(2,1)}), bf16[2048,5120]{1,0:T(8,128)(2,1)}) %all-gather.18.cloned.1.call-update) | async-done | bytes 20971536 | tf_op jit(solution)/shard_map/all_gather | solution.py:164
  521.7 12.6 fusion.110
  534.3 172.5 %all-gather.20.cloned.1.call-done = bf16[2048,5120]{1,0:T(8,128)(2,1)} async-done(((bf16[256,5120]{1,0:T(8,128)(2,1)}), bf16[2048,5120]{1,0:T(8,128)(2,1)}) %all-gather.20.cloned.1.call-update) | async-done | bytes 20971536 | tf_op jit(solution)/shard_map/all_gather | solution.py:165
  706.9 12.6 fusion.111
  719.5 172.7 %all-gather.22.cloned.1.call-done = bf16[2048,5120]{1,0:T(8,128)(2,1)} async-done(((bf16[256,5120]{1,0:T(8,128)(2,1)}), bf16[2048,5120]{1,0:T(8,128)(2,1)}) %all-gather.22.cloned.1.call-update) | async-done | bytes 20971536 | tf_op jit(solution)/shard_map/all_gather | solution.py:175
  892.2 15.9 multiply_convert_fusion.1
  920.3 13.3 multiply_reduce_fusion.3
  933.6 13.5 multiply_reduce_fusion.1
  959.4 14.3 all-to-all-done.4
  983.7 299.4 %while.75 = (s32[]{:T(128)}, f32[1024,8,64]{0,2,1:T(8,128)S(1)}, f32[1024,8,64]{0,2,1:T(8,128)}, f32[32,8]{0,1:T(8,128)S(1)}, bf16[2,512,8,64]{1,3,2,0:T(8,128)(...) while((s32[]{:T(128)}, f32[1024,8,64]{0,2,1:T(8,128)S(1)}, ...), condition=%wide.region_15.16_spmd.clone, body=%wide.region_9.15_spmd.clone.sunk | while | flops 2874930432 | bytes 288065920 | solution.py:239
  1002.5 32.4 %while.77 = (s32[]{:T(128)}, f32[8,512,1024]{2,1,0:T(8,128)}, s32[]{:T(128)}, bf16[32,8]{0,1:T(8,128)(2,1)S(1)}, s32[]{:T(128)}, /*index=5*/s32[]{:T(128)}, s32[]{:T(128)}, s32[]{:T(128)}) while((s32[]{:T(128)}, f32[8,512,1024]{2,1,0:T(8,128)}, s32[]{:T(128)}, bf16[32,8]{0,1:T(8,128)(2,1)S(1)}, s32[]{:T(128)}, /*index=5*/s32[]{:T(128)}, ...), condition=%wide.region_11.11_spmd, body=%wide.region_10.10_spmd.sunk | while | flops 74973320 | bytes 13633183 | solution.py:44
  1037.9 19.4 multiply_reduce_fusion.11
  1057.3 14.9 multiply_convert_fusion.5
  1084.5 41.0 %while.78 = (s32[]{:T(128)}, f32[32,8]{0,1:T(8,128)S(1)}, s32[]{:T(128)}, bf16[8,512,1024]{2,1,0:T(8,128)(2,1)}, s32[]{:T(128)}, /*index=5*/s32[]{:T(128)}, s32[]{:T(128)}, s32[]{:T(128)}) while((s32[]{:T(128)}, f32[32,8]{0,1:T(8,128)S(1)}, s32[]{:T(128)}, bf16[8,512,1024]{2,1,0:T(8,128)(2,1)}, s32[]{:T(128)}, ...), condition=%wide.region_14.14_spmd.clone, body=%wide.region_13.13_spmd.clone.sunk | while | flops 74973832 | bytes 11537577 | solution.py:64
  1151.1 32.4 %while.77 = (s32[]{:T(128)}, f32[8,512,1024]{2,1,0:T(8,128)}, s32[]{:T(128)}, bf16[32,8]{0,1:T(8,128)(2,1)S(1)}, s32[]{:T(128)}, /*index=5*/s32[]{:T(128)}, s32[]{:T(128)}, s32[]{:T(128)}) while((s32[]{:T(128)}, f32[8,512,1024]{2,1,0:T(8,128)}, s32[]{:T(128)}, bf16[32,8]{0,1:T(8,128)(2,1)S(1)}, s32[]{:T(128)}, /*index=5*/s32[]{:T(128)}, ...), condition=%wide.region_11.11_spmd, body=%wide.region_10.10_spmd.sunk | while | flops 74973320 | bytes 13633183 | solution.py:44
  1186.6 19.4 multiply_reduce_fusion.11
  1205.9 14.9 multiply_convert_fusion.5
  1234.7 41.0 %while.78 = (s32[]{:T(128)}, f32[32,8]{0,1:T(8,128)S(1)}, s32[]{:T(128)}, bf16[8,512,1024]{2,1,0:T(8,128)(2,1)}, s32[]{:T(128)}, /*index=5*/s32[]{:T(128)}, s32[]{:T(128)}, s32[]{:T(128)}) while((s32[]{:T(128)}, f32[32,8]{0,1:T(8,128)S(1)}, s32[]{:T(128)}, bf16[8,512,1024]{2,1,0:T(8,128)(2,1)}, s32[]{:T(128)}, ...), condition=%wide.region_14.14_spmd.clone, body=%wide.region_13.13_spmd.clone.sunk | while | flops 74973832 | bytes 11537577 | solution.py:64
  1356.3 12.5 copy.134
  1368.8 12.4 copy.135
  1396.6 12.4 copy.136
  1469.9 914.5 %reduce-scatter.4.cloned.1.call-done = bf16[256,23552]{1,0:T(8,128)(2,1)} async-done(((bf16[2048,23552]{1,0:T(8,128)(2,1)}), bf16[256,23552]{1,0:T(8,128)(2,1)}) %reduce-scatter.4.cloned.1.call-update) | async-done | bytes 12058640
  2407.7 45.0 %all-reduce.1 = (f32[2048]{0:T(1024)S(1)}, f32[32,32]{1,0:T(8,128)}, f32[2048]{0:T(1024)S(1)}, f32[4]{0:T(128)S(1)}, f32[]{:T(128)}) all-reduce(f32[2048]{0:T(1024)S(1)} %get-tuple-element.569, f32[32,32]{1,0:T(8,128)S(1)} %dynamic_update_slice.28, f32[2048]{0:T(1024)S(1)} %copy-done.30, ...), channel_id=1, replica_groups=mesh['seq'=4,'fsdp'=8] {'seq','fsdp'}, use_global_device_ids=true, to_apply=%region_18.19 | all-reduce | flops 5125 | bytes 41000 | tf_op jit(solution)/shard_map/psum | solution.py:304
  2458.4 163.0 %all-reduce.4.cloned.1.call-done = bf16[256,23552]{1,0:T(8,128)(2,1)} async-done(((bf16[256,23552]{1,0:T(8,128)(2,1)}), bf16[256,23552]{1,0:T(8,128)(2,1)}) %all-reduce.4.cloned.1.call-update) | async-done | bytes 12058640 | tf_op jit(solution)/shard_map/psum | solution.py:292
  (358 shorter events, 668.6 us)
Async XLA Ops:
  7.2 258.5 %copy-start = (bf16[32,32]{1,0:T(8,128)(2,1)S(1)}, bf16[32,32]{1,0:T(8,128)(2,1)}, u32[]{:S(2)}) copy-start(bf16[32,32]{1,0:T(8,128)(2,1)} %param.33) | copy-start | bytes 6148
  7.2 83.0 %all-gather.10.cloned.1.call-start = ((), (), s32[]{:S(2)}) async-start(), calls=%async_computation.9 | async-start | bytes 9437184 | tf_op jit(solution)/shard_map/all_gather | solution.py:112
  7.9 164.4 %all-gather.12.cloned.1.call-start = ((), (), s32[]{:S(2)}) async-start(), calls=%async_computation.10 | async-start | bytes 9437184 | tf_op jit(solution)/shard_map/all_gather | solution.py:113
  8.7 245.8 %all-gather.14.cloned.1.call-start = ((), (), s32[]{:S(2)}) async-start(), calls=%async_computation.11 | async-start | bytes 9437184 | tf_op jit(solution)/shard_map/all_gather | solution.py:114
  9.4 460.2 %all-gather.16.cloned.1.call-start = ((), (), s32[]{:S(2)}) async-start(), calls=%async_computation.12 | async-start | bytes 9437184 | tf_op jit(solution)/shard_map/all_gather | solution.py:115
  10.0 511.7 %all-gather.18.cloned.1.call-start = ((), (), s32[]{:S(2)}) async-start(), calls=%async_computation.13 | async-start | bytes 23592960 | tf_op jit(solution)/shard_map/all_gather | solution.py:164
  10.6 696.3 %all-gather.20.cloned.1.call-start = ((), (), s32[]{:S(2)}) async-start(), calls=%async_computation.14 | async-start | bytes 23592960 | tf_op jit(solution)/shard_map/all_gather | solution.py:165
  11.2 881.0 %all-gather.22.cloned.1.call-start = ((), (), s32[]{:S(2)}) async-start(), calls=%async_computation.15 | async-start | bytes 23592960 | tf_op jit(solution)/shard_map/all_gather | solution.py:175
  21.0 233.4 %copy-start.23 = (f32[8,1,256]{2,1,0:T(1,128)}, f32[8,1,256]{2,1,0:T(1,128)S(1)}, u32[]{:S(2)}) copy-start(f32[8,1,256]{2,1,0:T(1,128)S(1)} %convert_element_type.389) | copy-start | bytes 24580
  21.3 68.8 %copy-start.28 = (f32[256]{0:T(256)}, f32[256]{0:T(256)S(1)}, u32[]{:S(2)}) copy-start(f32[256]{0:T(256)S(1)} %fusion.85) | copy-start | bytes 3076
  21.4 233.1 %copy-start.26 = (f32[256]{0:T(256)}, f32[256]{0:T(256)S(1)}, u32[]{:S(2)}) copy-start(f32[256]{0:T(256)S(1)} %add_rsqrt_fusion.1) | copy-start | bytes 3076
  97.3 81.9 %all-to-all-start = ((bf16[256,4,512]{0,2,1:T(8,128)(2,1)}), bf16[256,4,512]{0,2,1:T(8,128)(2,1)S(1)}, u32[]{:S(2)}, u32[]{:S(2)}) async-start(bf16[256,4,512]{0,2,1:T(8,128)(2,1)} %bitcast.13), calls=%async_computation | async-start | bytes 2097152 | tf_op jit(solution)/shard_map/all_to_all | solution.py:126
  179.2 82.2 %all-to-all-start.1 = ((bf16[256,4,512]{2,0,1:T(8,128)(2,1)}), bf16[256,4,512]{2,0,1:T(8,128)(2,1)S(1)}, u32[]{:S(2)}, u32[]{:S(2)}) async-start(bf16[256,4,512]{2,0,1:T(8,128)(2,1)} %bitcast.259), calls=%async_computation.1 | async-start | bytes 2097152 | tf_op jit(solution)/shard_map/all_to_all | solution.py:127
  261.3 18.7 all-to-all-start.2
  268.1 17.2 copy-start.22
  330.0 19.7 copy-start.16
  404.8 19.2 copy-start.16
  432.2 45.3 %copy-start.6 = (bf16[1024,8,64]{0,2,1:T(8,128)(2,1)}, bf16[1024,8,64]{0,2,1:T(8,128)(2,1)S(1)}, u32[]{:S(2)}) copy-start(bf16[1024,8,64]{0,2,1:T(8,128)(2,1)S(1)} %get-tuple-element.1152) | copy-start | bytes 3145732
  432.2 45.3 %copy-start.8 = (bf16[1024,8,64]{0,2,1:T(8,128)(2,1)}, bf16[1024,8,64]{0,2,1:T(8,128)(2,1)S(1)}, u32[]{:S(2)}) copy-start(bf16[1024,8,64]{0,2,1:T(8,128)(2,1)S(1)} %get-tuple-element.1153) | copy-start | bytes 3145732
  432.2 45.3 %copy-start.9 = (bf16[2,512,8,64]{1,3,2,0:T(8,128)(2,1)}, bf16[2,512,8,64]{1,3,2,0:T(8,128)(2,1)S(1)}, u32[]{:S(2)}) copy-start(bf16[2,512,8,64]{1,3,2,0:T(8,128)(2,1)S(1)} %get-tuple-element.1154) | copy-start | bytes 3145732
  432.2 25.0 copy-start.39
  452.9 17.3 all-to-all-start.3
  479.0 227.9 %copy-start.20 = (bf16[256,2048]{1,0:T(8,128)(2,1)}, bf16[256,2048]{1,0:T(8,128)(2,1)S(1)}, u32[]{:S(2)}) copy-start(bf16[256,2048]{1,0:T(8,128)(2,1)S(1)} %multiply_convert_fusion.3) | copy-start | bytes 3145732
  534.3 357.9 %copy-start.36 = (bf16[1,256,2048]{2,1,0:T(8,128)(2,1)S(1)}, bf16[1,256,2048]{2,1,0:T(8,128)(2,1)}, u32[]{:S(2)}) copy-start(bf16[1,256,2048]{2,1,0:T(8,128)(2,1)} %param.25) | copy-start | bytes 3145732
  955.0 28.7 %copy-start.7 = (bf16[1024,8,64]{0,2,1:T(8,128)(2,1)S(1)}, bf16[1024,8,64]{0,2,1:T(8,128)(2,1)}, u32[]{:S(2)}) copy-start(bf16[1024,8,64]{0,2,1:T(8,128)(2,1)} %copy-done.6) | copy-start | bytes 3145732
  955.0 18.8 all-to-all-start.4
  1289.0 17.8 all-to-all-start.5
  1294.4 16.6 copy-start.14
  1306.7 38.2 %all-to-all-start.6 = ((bf16[4,256,512]{1,2,0:T(8,128)(2,1)}), bf16[4,256,512]{1,2,0:T(8,128)(2,1)}, u32[]{:S(2)}, u32[]{:S(2)}) async-start(bf16[4,256,512]{1,2,0:T(8,128)(2,1)} %copy.131), calls=%async_computation.6 | async-start | bytes 2097152 | tf_op jit(solution)/shard_map/all_to_all | solution.py:249
  1344.9 44.7 %all-to-all-start.7 = ((bf16[4,256,512]{1,2,0:T(8,128)(2,1)}), bf16[4,256,512]{1,2,0:T(8,128)(2,1)}, u32[]{:S(2)}, u32[]{:S(2)}) async-start(bf16[4,256,512]{1,2,0:T(8,128)(2,1)} %copy.132), calls=%async_computation.7 | async-start | bytes 2097152 | tf_op jit(solution)/shard_map/all_to_all | solution.py:250
  1349.2 1035.3 %reduce-scatter.4.cloned.1.call-start = ((), (), s32[]{:S(2)}) async-start(), calls=%async_computation.17 | async-start | bytes 108527616
  1469.9 1151.6 %all-reduce.4.cloned.1.call-start = ((), (), s32[]{:S(2)}) async-start(), calls=%async_computation.16 | async-start | bytes 24117248 | tf_op jit(solution)/shard_map/psum | solution.py:292
  (36 other events, 250.7 us)
Sparse Core Ops, SparseCore 0:
  9.6 80.5 all-gather.9
  91.8 80.5 all-gather.11
  173.9 80.5 all-gather.13
  255.9 80.5 all-gather.15
  338.0 183.6 all-gather.17
  523.2 183.6 all-gather.19
  708.5 183.6 all-gather.21
  1470.0 914.4 reduce-scatter.3
  2388.0 233.3 all-reduce.3
where the time goes:
time: 2660 us; the launch traced here: 2640 us
  waiting for transfers between devices  1720 us (65%)
  matrix products  389 us (15%)
  local copies, waits for them, and re-layouts  324 us (12%)
  other arithmetic  77.1 us (3%)
  blocking collectives  66.4 us (2%)
  starting transfers between devices  33.8 us (1%)
    unnamed x10, waiting for transfers between devices  919 us
    all_gather x1, waiting for transfers between devices, on_device(): lax.all_gather(w_down, 'fsdp', axis=0, tiled=True)  173 us
    all_gather x1, waiting for transfers between devices, on_device(): up_piece = lax.all_gather(w_up, 'fsdp', axis=0, tiled=True)  173 us
    psum x1, waiting for transfers between devices, on_device(): lax.psum(summed_rows.astype(jnp.bfloat16), 'seq').astype(jnp.float32)  163 us
    another operation x10, local copies, waits for them, and re-layouts  83.4 us
    all_gather x1, waiting for transfers between devices, on_device(): value_piece = lax.all_gather(w_value, 'fsdp', axis=0, tiled=True)  71.5 us
    all_gather x1, waiting for transfers between devices, on_device(): key_piece = lax.all_gather(w_key, 'fsdp', axis=0, tiled=True)  71.2 us
    dynamic_update_slice x16, local copies, waits for them, and re-layouts, block_add_piece(): return lax.dynamic_update_slice_in_dim(filled, part_bias, offset, 1)  70.6 us
  transfers between devices with their start and end apart: 17, of which 12 were waited for; matrix products, arithmetic and copies ran while one was open for 12% of the time, Pallas kernels for 0%

commit v1 on v0

v1 whole, which is shorter than its diff:
```python
import jax
import jax.numpy as jnp
from jax import lax
from jax.experimental import pallas as pl
from jax.experimental.pallas import tpu as pltpu
from jax.sharding import PartitionSpec as P

DH = 64
LANES = 128
BLOCK = 128
NEAR = 3 * BLOCK
PAD = 2 * BLOCK

epsilon = 1e-06
masked_score = -1e30
far_steps = (12, 16, 23, 32, 46, 64, 91)
FAR_BUCKET = 8 + len(far_steps)

bf16 = jnp.bfloat16
f32 = jnp.float32


def bucket_of(relative):
    distance = jnp.abs(relative)
    far_bucket = jnp.full(relative.shape, 8, jnp.int32)
    for threshold in far_steps:
        far_bucket = far_bucket + (distance >= threshold).astype(jnp.int32)
    near_bucket = jnp.where(distance < 8, distance, far_bucket)
    return near_bucket + 16 * (relative > 0).astype(jnp.int32)


def near_onehot(buckets):
    key_pos = jnp.arange(NEAR, dtype=jnp.int32) - BLOCK
    query_pos = jnp.arange(BLOCK, dtype=jnp.int32)
    labels = bucket_of(key_pos[:, None] - query_pos[None, :])
    return labels[:, :, None] == jnp.arange(buckets, dtype=jnp.int32)


def swap(value, distance):
    return lax.ppermute(value, "seq", [(rank, rank ^ distance) for rank in range(4)])


def seq_gather(own):
    half = own.shape[0] // 2
    one, two = swap(own, 1), swap(own, 2)
    return [own, one, two, swap(one[:half], 2), swap(two[half:], 1)]


def seq_scatter_sum(rows):
    count = rows.shape[0] // 4
    half = count // 2

    def piece(chunk, second):
        start = chunk * count + second * half
        return rows[start : start + half]

    def add(left, right):
        return left.astype(f32) + right.astype(f32)

    got_one = swap(jnp.concatenate([piece(3, 0), piece(1, 0)]), 1)
    got_two = swap(jnp.concatenate([piece(3, 1), piece(2, 1)]), 2)
    first_out = add(piece(2, 0), got_one[:half]).astype(bf16)
    second_out = add(piece(1, 1), got_two[:half]).astype(bf16)
    first_in = swap(first_out, 2)
    second_in = swap(second_out, 1)
    first = add(add(piece(0, 0), got_one[half:]), first_in)
    second = add(add(piece(0, 1), got_two[half:]), second_in)
    return jnp.concatenate([first, second])


def sum_everywhere(value, axis_sizes):
    for name, size in axis_sizes:
        step = 1
        while step < size:
            value = value + lax.ppermute(value, name, [(i, i ^ step) for i in range(size)])
            step *= 2
    return value


def column_pick(rank, arrays, build, out_widths, parts):
    rows = arrays[0].shape[0]
    width = [a.shape[1] // parts for a in arrays]
    return pl.pallas_call(
        build,
        out_shape=[jax.ShapeDtypeStruct((rows, w), bf16) for w in out_widths],
        grid_spec=pltpu.PrefetchScalarGridSpec(
            num_scalar_prefetch=1,
            grid=(1,),
            in_specs=[pl.BlockSpec((rows, w), lambda i, r: (0, r[0])) for w in width],
            out_specs=[pl.BlockSpec((rows, w), lambda i, r: (0, 0)) for w in out_widths],
        ),
        name="column_pick",
    )(rank, *arrays)


def pick_attention(rank_ref, q_ref, k_ref, v_ref, o_ref, out_ref):
    width = q_ref.shape[1]
    for pair in range(width // LANES):
        for which, ref in enumerate((q_ref, k_ref, v_ref)):
            start = (3 * pair + which) * LANES
            out_ref[:, start : start + LANES] = ref[:, pair * LANES : (pair + 1) * LANES]
    out_ref[:, 3 * width :] = o_ref[...]


def pick_hidden(rank_ref, g_ref, u_ref, d_ref, gu_ref, down_ref):
    width = g_ref.shape[1]
    gu_ref[:, :width] = g_ref[...]
    gu_ref[:, width:] = u_ref[...]
    down_ref[...] = d_ref[...]


def column_place(rank, pieces, out_count, store):
    rows, width = pieces[0].shape
    half = rows // 2
    out_width = width // out_count

    def body(rank_ref, own_ref, one_ref, two_ref, lo_ref, hi_ref, *out_refs):
        distance = pl.program_id(0) ^ rank_ref[0]
        for index, ref in enumerate((own_ref, one_ref, two_ref)):

            @pl.when(distance == index)
            def _(ref=ref):
                store(ref, out_refs, slice(0, rows))

        @pl.when(distance == 3)
        def _():
            store(lo_ref, out_refs, slice(0, half))
            store(hi_ref, out_refs, slice(half, rows))

    return pl.pallas_call(
        body,
        out_shape=[jax.ShapeDtypeStruct((rows, 4 * out_width), f32)] * out_count,
        grid_spec=pltpu.PrefetchScalarGridSpec(
            num_scalar_prefetch=1,
            grid=(4,),
            in_specs=[pl.BlockSpec(p.shape, lambda q, r: (0, 0)) for p in pieces],
            out_specs=[pl.BlockSpec((rows, out_width), lambda q, r: (0, q))] * out_count,
        ),
        name="column_place",
    )(rank, *pieces)


def store_plain(ref, out_refs, rows):
    width = out_refs[0].shape[1]
    for index, out in enumerate(out_refs):
        out[rows, :] = ref[:, index * width : (index + 1) * width].astype(f32)


def store_pairs(ref, out_refs, rows):
    for pair in range(out_refs[0].shape[1] // LANES):
        for which, out in enumerate(out_refs):
            start = (3 * pair + which) * LANES
            out[rows, pair * LANES : (pair + 1) * LANES] = ref[:, start : start + LANES].astype(f32)


def matmul_nt(left, right):
    return lax.dot_general(
        left, right, (((1,), (1,)), ((), ())), preferred_element_type=f32
    )


def matmul_nn(left, right):
    return jnp.dot(left, right, preferred_element_type=f32)


def two_heads(rows):
    lane = lax.broadcasted_iota(jnp.int32, rows.shape, 1)
    none = jnp.zeros_like(rows)
    return jnp.concatenate(
        [jnp.where(lane < DH, rows, none), jnp.where(lane < DH, none, rows)], axis=0
    )


def one_pair(columns):
    count = columns.shape[1] // 2
    left, right = columns[:, :count], columns[:, count:]
    row = lax.broadcasted_iota(jnp.int32, left.shape, 0)
    return jnp.where(row < DH, left, right).T


def held_at(rank_ref, block, per_chunk):
    chunk = (block // per_chunk) ^ rank_ref[0]
    return pl.multiple_of((chunk * per_chunk + block % per_chunk) * BLOCK, BLOCK)


def far_is_live(seg_ref, block, blocks, side):
    other = block + 2 * side
    inside = jnp.logical_and(other >= 0, other < blocks)
    other = jnp.clip(other, 0, blocks - 1)
    if side < 0:
        same = seg_ref[other * BLOCK + BLOCK - 1] == seg_ref[block * BLOCK]
    else:
        same = seg_ref[other * BLOCK] == seg_ref[block * BLOCK + BLOCK - 1]
    return jnp.logical_and(inside, same)


def forward_kernel(
    rank_ref, seg_ref, qkv_ref, bias_ref, far_ref, key_seg_ref, query_seg_ref,
    out_ref, log_ref, k_ref, vt_ref, top_ref, total_ref, acc_ref, *, per_chunk,
):
    length = qkv_ref.shape[0]
    blocks = length // BLOCK
    for edge in (0, PAD + length):
        k_ref[edge : edge + PAD, :] = jnp.zeros((PAD, LANES), bf16)
        vt_ref[:, edge : edge + PAD] = jnp.zeros((LANES, PAD), bf16)
    for block in range(blocks):
        row = held_at(rank_ref, block, per_chunk)
        start = PAD + block * BLOCK
        k_ref[start : start + BLOCK, :] = qkv_ref[pl.ds(row, BLOCK), LANES : 2 * LANES]
        vt_ref[:, start : start + BLOCK] = qkv_ref[pl.ds(row, BLOCK), 2 * LANES :].T

    def one_block(block, carry):
        row = held_at(rank_ref, block, per_chunk)
        query = two_heads(qkv_ref[pl.ds(row, BLOCK), :LANES])
        query_seg = query_seg_ref[pl.ds(block, 1), :]

        def scores_at(start, count, bias):
            scores = matmul_nt(k_ref[pl.ds(start, count), :], query) + bias
            key_seg = key_seg_ref[pl.ds(start, count), :]
            same = jnp.concatenate([key_seg, key_seg], axis=1) == query_seg
            return jnp.where(same, scores, masked_score)

        start = pl.multiple_of(PAD - BLOCK + block * BLOCK, BLOCK)
        scores = scores_at(start, NEAR, bias_ref[0])
        top = jnp.max(scores, axis=0, keepdims=True)
        expo = jnp.exp(scores - top)
        top_ref[...] = top
        total_ref[...] = jnp.sum(expo, axis=0, keepdims=True)
        acc_ref[...] = matmul_nn(vt_ref[:, pl.ds(start, NEAR)], expo.astype(bf16))

        for index, side in enumerate((-1, 1)):

            @pl.when(far_is_live(seg_ref, block, blocks, side))
            def _(index=index, side=side):
                start = pl.multiple_of(PAD + (block + 2 * side) * BLOCK, BLOCK)
                scores = scores_at(start, BLOCK, far_ref[0, index : index + 1, :])
                old_top = top_ref[...]
                top = jnp.maximum(old_top, jnp.max(scores, axis=0, keepdims=True))
                scale = jnp.exp(old_top - top)
                expo = jnp.exp(scores - top)
                top_ref[...] = top
                total_ref[...] = total_ref[...] * scale + jnp.sum(expo, axis=0, keepdims=True)
                acc_ref[...] = acc_ref[...] * scale + matmul_nn(
                    vt_ref[:, pl.ds(start, BLOCK)], expo.astype(bf16)
                )

        total = total_ref[...]
        out_ref[pl.ds(row, BLOCK), :] = one_pair(acc_ref[...] / total).astype(bf16)
        log_ref[0, pl.ds(block, 1), :] = top_ref[...] + jnp.log(total)
        return carry

    lax.fori_loop(0, blocks, one_block, 0)


def backward_kernel(
    rank_ref, seg_ref, qkv_ref, out_ref, dout_ref, log_ref, bias_ref, far_ref, key_seg_ref,
    query_seg_ref, grad_ref, near_grad_ref, far_grad_ref,
    k_ref, kt_ref, v_ref, dk_ref, dv_ref, dq_ref, *, per_chunk,
):
    length = qkv_ref.shape[0]
    blocks = length // BLOCK
    for edge in (0, PAD + length):
        k_ref[edge : edge + PAD, :] = jnp.zeros((PAD, LANES), bf16)
        kt_ref[:, edge : edge + PAD] = jnp.zeros((LANES, PAD), bf16)
        v_ref[edge : edge + PAD, :] = jnp.zeros((PAD, LANES), bf16)
    for block in range(blocks):
        row = held_at(rank_ref, block, per_chunk)
        start = PAD + block * BLOCK
        key = qkv_ref[pl.ds(row, BLOCK), LANES : 2 * LANES]
        k_ref[start : start + BLOCK, :] = key
        kt_ref[:, start : start + BLOCK] = key.T
        v_ref[start : start + BLOCK, :] = qkv_ref[pl.ds(row, BLOCK), 2 * LANES :]
    dk_ref[...] = jnp.zeros_like(dk_ref)
    dv_ref[...] = jnp.zeros_like(dv_ref)
    near_grad_ref[...] = jnp.zeros_like(near_grad_ref)
    far_grad_ref[...] = jnp.zeros_like(far_grad_ref)

    def one_block(block, carry):
        row = held_at(rank_ref, block, per_chunk)
        query = two_heads(qkv_ref[pl.ds(row, BLOCK), :LANES])
        dout_rows = dout_ref[pl.ds(row, BLOCK), :]
        dout = two_heads(dout_rows)
        query_seg = query_seg_ref[pl.ds(block, 1), :]
        log_row = log_ref[0, pl.ds(block, 1), :]
        product = (dout_rows.astype(f32) * out_ref[pl.ds(row, BLOCK), :].astype(f32)).T
        row_dot = jnp.concatenate(
            [
                jnp.sum(product[:DH], axis=0, keepdims=True),
                jnp.sum(product[DH:], axis=0, keepdims=True),
            ],
            axis=1,
        )

        def d_scores_at(start, count, bias):
            scores = matmul_nt(k_ref[pl.ds(start, count), :], query) + bias
            key_seg = key_seg_ref[pl.ds(start, count), :]
            same = jnp.concatenate([key_seg, key_seg], axis=1) == query_seg
            prob = jnp.exp(jnp.where(same, scores, masked_score) - log_row)
            d_prob = matmul_nt(v_ref[pl.ds(start, count), :], dout)
            d_scores = prob * (d_prob - row_dot)
            low = d_scores.astype(bf16)
            dk_ref[pl.ds(start, count), :] += matmul_nn(low, query)
            dv_ref[pl.ds(start, count), :] += matmul_nn(prob.astype(bf16), dout)
            return d_scores, matmul_nn(kt_ref[:, pl.ds(start, count)], low)

        start = pl.multiple_of(PAD - BLOCK + block * BLOCK, BLOCK)
        d_scores, d_query = d_scores_at(start, NEAR, bias_ref[0])
        near_grad_ref[0] += d_scores
        dq_ref[...] = d_query
        for index, side in enumerate((-1, 1)):

            @pl.when(far_is_live(seg_ref, block, blocks, side))
            def _(index=index, side=side):
                start = pl.multiple_of(PAD + (block + 2 * side) * BLOCK, BLOCK)
                d_scores, d_query = d_scores_at(start, BLOCK, far_ref[0, index : index + 1, :])
                far_grad_ref[0, index : index + 1, :] += jnp.sum(d_scores, axis=0, keepdims=True)
                dq_ref[...] += d_query

        grad_ref[pl.ds(row, BLOCK), :LANES] = one_pair(dq_ref[...]).astype(bf16)
        return carry

    lax.fori_loop(0, blocks, one_block, 0)
    for block in range(blocks):
        row = held_at(rank_ref, block, per_chunk)
        start = PAD + block * BLOCK
        grad_ref[pl.ds(row, BLOCK), LANES : 2 * LANES] = dk_ref[start : start + BLOCK, :].astype(bf16)
        grad_ref[pl.ds(row, BLOCK), 2 * LANES :] = dv_ref[start : start + BLOCK, :].astype(bf16)


def attention_specs(length, blocks):
    whole = lambda p, *_: (0, 0)
    return {
        "qkv": pl.BlockSpec((length, 3 * LANES), lambda p, *_: (0, p)),
        "head": pl.BlockSpec((length, LANES), lambda p, *_: (0, p)),
        "log": pl.BlockSpec((1, blocks, 2 * BLOCK), lambda p, *_: (p, 0, 0)),
        "bias": pl.BlockSpec((1, NEAR, 2 * BLOCK), lambda p, *_: (p, 0, 0)),
        "far": pl.BlockSpec((1, 8, 2 * BLOCK), lambda p, *_: (p, 0, 0)),
        "key_seg": pl.BlockSpec((length + 2 * PAD, LANES), whole),
        "query_seg": pl.BlockSpec((blocks, 2 * BLOCK), whole),
    }


def attention_forward(rank, seg_row, qkv, bias):
    length = qkv.shape[0]
    blocks, pairs = length // BLOCK, qkv.shape[1] // (3 * LANES)
    spec = attention_specs(length, blocks)
    padded = (length + 2 * PAD, LANES)

    def body(*refs):
        forward_kernel(*refs, per_chunk=blocks // 4)

    return pl.pallas_call(
        body,
        out_shape=[
            jax.ShapeDtypeStruct((length, pairs * LANES), bf16),
            jax.ShapeDtypeStruct((pairs, blocks, 2 * BLOCK), f32),
        ],
        grid_spec=pltpu.PrefetchScalarGridSpec(
            num_scalar_prefetch=2,
            grid=(pairs,),
            in_specs=[spec[n] for n in ("qkv", "bias", "far", "key_seg", "query_seg")],
            out_specs=[spec["head"], spec["log"]],
            scratch_shapes=[
                pltpu.VMEM(padded, bf16),
                pltpu.VMEM(padded[::-1], bf16),
                pltpu.VMEM((1, 2 * BLOCK), f32),
                pltpu.VMEM((1, 2 * BLOCK), f32),
                pltpu.VMEM((LANES, 2 * BLOCK), f32),
            ],
        ),
        name="attention_forward",
    )(rank, seg_row, qkv, *bias)


def attention_backward(rank, seg_row, qkv, context, d_context, logs, bias):
    length = qkv.shape[0]
    blocks, pairs = length // BLOCK, qkv.shape[1] // (3 * LANES)
    spec = attention_specs(length, blocks)
    padded = (length + 2 * PAD, LANES)

    def body(*refs):
        backward_kernel(*refs, per_chunk=blocks // 4)

    names = ("qkv", "head", "head", "log", "bias", "far", "key_seg", "query_seg")
    return pl.pallas_call(
        body,
        out_shape=[
            jax.ShapeDtypeStruct(qkv.shape, bf16),
            jax.ShapeDtypeStruct((pairs, NEAR, 2 * BLOCK), f32),
            jax.ShapeDtypeStruct((pairs, 8, 2 * BLOCK), f32),
        ],
        grid_spec=pltpu.PrefetchScalarGridSpec(
            num_scalar_prefetch=2,
            grid=(pairs,),
            in_specs=[spec[n] for n in names],
            out_specs=[spec["qkv"], spec["bias"], spec["far"]],
            scratch_shapes=[
                pltpu.VMEM(padded, bf16),
                pltpu.VMEM(padded[::-1], bf16),
                pltpu.VMEM(padded, bf16),
                pltpu.VMEM(padded, f32),
                pltpu.VMEM(padded, f32),
                pltpu.VMEM((LANES, 2 * BLOCK), f32),
            ],
        ),
        name="attention_backward",
    )(rank, seg_row, qkv, context, d_context, logs, *bias)


def bias_operands(table, seg_row):
    buckets, heads = table.shape
    pairs = heads // 2
    near = jnp.einsum(
        "jik,kh->hji", near_onehot(buckets).astype(bf16), table, preferred_element_type=f32
    )
    near = near.reshape(pairs, 2, NEAR, BLOCK).transpose(0, 2, 1, 3).reshape(pairs, NEAR, 2 * BLOCK)
    ends = jnp.stack([table[FAR_BUCKET], table[FAR_BUCKET + 16]]).astype(f32)
    ends = ends.reshape(2, pairs, 2).transpose(1, 0, 2)
    far = jnp.broadcast_to(ends[:, :, :, None], (pairs, 2, 2, BLOCK)).reshape(pairs, 2, 2 * BLOCK)
    far = jnp.pad(far, ((0, 0), (0, 6), (0, 0)))
    key_seg = jnp.broadcast_to(
        jnp.pad(seg_row, (PAD, PAD), constant_values=-1)[:, None], (seg_row.shape[0] + 2 * PAD, LANES)
    )
    rows = seg_row.reshape(-1, BLOCK)
    return near, far, key_seg, jnp.concatenate([rows, rows], axis=1)


def table_grad(near_grad, far_grad, buckets):
    pairs = near_grad.shape[0]
    near = near_grad.reshape(pairs, NEAR, 2, BLOCK)
    table = jnp.einsum(
        "pjhi,jik->kph", near, near_onehot(buckets).astype(f32), precision=lax.Precision.HIGHEST
    ).reshape(buckets, 2 * pairs)
    far = jnp.sum(far_grad.reshape(pairs, 8, 2, BLOCK), axis=-1)
    for index, bucket in enumerate((FAR_BUCKET, FAR_BUCKET + 16)):
        table = table.at[bucket].add(far[:, index].reshape(2 * pairs))
    return table


def tanh_parts(gate):
    inner = 0.7978845608028654 * (gate + 0.044715 * gate * gate * gate)
    slope = 0.7978845608028654 * (1.0 + 3.0 * 0.044715 * gate * gate)
    return jnp.tanh(inner), slope


def on_device(
    inputs,
    cotangent,
    segments,
    valid,
    norm_attn,
    query_weight,
    w_key,
    w_value,
    w_out,
    rel_bias,
    norm_ff,
    w_gate,
    w_up,
    w_down,
    *,
    axis_sizes,
):
    seq_index = lax.axis_index("seq")
    rank = seq_index.reshape(1).astype(jnp.int32)
    shard_rows, model_width = query_weight.shape
    hidden_units = w_gate.shape[1]
    parts = dict(axis_sizes)["seq"]
    attn_part = model_width // parts
    hidden_part = hidden_units // parts
    heads_local = attn_part // DH
    seg_row = segments[0]
    x_low, grad_low = inputs[0], cotangent[0]
    x_in = x_low.astype(f32)

    (attn_own,) = column_pick(
        rank, (query_weight, w_key, w_value, w_out), pick_attention, (4 * attn_part,), parts
    )
    attn_weight = lax.all_gather(attn_own, "fsdp", axis=0, tiled=True)
    gu_own, down_own = column_pick(
        rank, (w_gate, w_up, w_down), pick_hidden, (2 * hidden_part, hidden_part), parts
    )
    gu_weight = lax.all_gather(gu_own, "fsdp", axis=0, tiled=True)
    down_weight = lax.all_gather(down_own, "fsdp", axis=0, tiled=True)
    gains = lax.all_gather(jnp.stack([norm_attn, norm_ff]), "fsdp", axis=1, tiled=True).astype(f32)
    gain_one, gain_two = gains[0:1], gains[1:2]
    qkv_weight, out_weight = attn_weight[:, : 3 * attn_part], attn_weight[:, 3 * attn_part :]

    def scale_of(rows):
        return lax.rsqrt(jnp.mean(rows * rows, axis=-1, keepdims=True) + epsilon)

    def gathered(own):
        return jnp.concatenate(seq_gather(own))

    def trans_dot(left_side, right_side):
        return lax.dot_general(
            left_side, right_side, (((0,), (0,)), ((), ())), preferred_element_type=f32
        ).astype(bf16)

    def over_shards(gradient):
        return lax.psum_scatter(gradient, "fsdp", scatter_dimension=0, tiled=True)

    x_all = gathered(x_low).astype(f32)
    normed_one = (x_all * scale_of(x_all) * gain_one).astype(bf16)
    table = lax.dynamic_slice_in_dim(rel_bias, seq_index * heads_local, heads_local, 1)
    bias = bias_operands(table, seg_row)
    qkv = jnp.dot(normed_one, qkv_weight, preferred_element_type=f32).astype(bf16)
    context, logs = attention_forward(rank, seg_row, qkv, bias)
    attn_out = seq_scatter_sum(matmul_nt(context, out_weight).astype(bf16))
    middle = x_in + attn_out
    scale_two = scale_of(middle)
    normed_two = gathered((middle * scale_two * gain_two).astype(bf16))
    grad_all = gathered(grad_low)
    gate_up = jnp.dot(normed_two, gu_weight, preferred_element_type=f32)
    gate, up_proj = gate_up[:, :hidden_part], gate_up[:, hidden_part:]
    bend, slope = tanh_parts(gate)
    act = 0.5 * gate * (1.0 + bend)
    hidden = lax.optimization_barrier((act * up_proj).astype(bf16))
    sum_down = over_shards(trans_dot(grad_all, hidden))
    ff_out = seq_scatter_sum(matmul_nt(hidden, down_weight).astype(bf16))
    output = (middle + ff_out).astype(bf16)[None]

    d_hidden = jnp.dot(grad_all, down_weight, preferred_element_type=f32)
    d_gate = d_hidden * up_proj * (0.5 * (1.0 + bend) + 0.5 * gate * (1.0 - bend * bend) * slope)
    d_gu = jnp.concatenate([d_gate.astype(bf16), (d_hidden * act).astype(bf16)], axis=1)
    d_normed_two = seq_scatter_sum(matmul_nt(d_gu, gu_weight).astype(bf16))
    sum_gu = over_shards(trans_dot(normed_two, d_gu))
    unit_two = d_normed_two * gain_two
    d_middle = (
        grad_low.astype(f32)
        + scale_two * unit_two
        - middle * scale_two**3 * jnp.mean(unit_two * middle, axis=-1, keepdims=True)
    )

    d_attn = gathered(d_middle.astype(bf16))
    d_context = jnp.dot(d_attn, out_weight, preferred_element_type=f32).astype(bf16)
    d_qkv, near_grad, far_grad = attention_backward(
        rank, seg_row, qkv, context, d_context, logs, bias
    )
    sum_qkv = over_shards(trans_dot(normed_one, d_qkv))
    sum_out = over_shards(trans_dot(d_attn, context))
    d_normed_one = seq_scatter_sum(matmul_nt(d_qkv, qkv_weight).astype(bf16))
    scale_one = scale_of(x_in)
    unit_one = d_normed_one * gain_one
    d_input = (
        d_middle
        + scale_one * unit_one
        - x_in * scale_one**3 * jnp.mean(unit_one * x_in, axis=-1, keepdims=True)
    )
    grad_inputs = d_input.astype(bf16)[None]

    (grad_down,) = column_place(rank, seq_gather(sum_down), 1, store_plain)
    grad_gate, grad_up = column_place(rank, seq_gather(sum_gu), 2, store_plain)
    (grad_out,) = column_place(rank, seq_gather(sum_out), 1, store_plain)
    grad_query, grad_key, grad_value = column_place(rank, seq_gather(sum_qkv), 3, store_pairs)

    def gain_grad(pairs, gain):
        total = sum(jnp.sum(weight.astype(f32) * grad, axis=1) for weight, grad in pairs)
        return total / gain.astype(f32)

    grad_norm_ff = gain_grad(((w_gate, grad_gate), (w_up, grad_up)), norm_ff)
    grad_norm_attn = gain_grad(
        ((query_weight, grad_query), (w_key, grad_key), (w_value, grad_value)), norm_attn
    )

    live_rows = valid[0].astype(f32)

    def live_sum(rows):
        return jnp.sum(live_rows * jnp.sum(rows * rows, axis=-1))

    stats = jnp.stack(
        [live_sum(x_in), live_sum(attn_out), live_sum(middle), live_sum(ff_out), jnp.sum(live_rows)]
    )
    d_table = table_grad(near_grad, far_grad, rel_bias.shape[0])
    table_full = lax.dynamic_update_slice_in_dim(
        jnp.zeros(rel_bias.shape, f32), d_table, seq_index * heads_local, 1
    )
    packed = jnp.concatenate([table_full, jnp.pad(stats, (0, table_full.shape[1] - 5))[None]])
    packed = sum_everywhere(packed, axis_sizes)
    table_sum, stat_sum = packed[:-1], packed[-1]
    rms_stats = jnp.sqrt(stat_sum[:4] / (stat_sum[4] * model_width))
    return (
        output,
        grad_inputs,
        grad_norm_attn,
        grad_query,
        grad_key,
        grad_value,
        grad_out,
        table_sum,
        grad_norm_ff,
        grad_gate,
        grad_up,
        grad_down,
        rms_stats,
    )


def solution(mesh):
    placed = (
        P("fsdp", "seq", None),
        P("fsdp", "seq", None),
        P("fsdp", None),
        P("fsdp", "seq"),
        P("fsdp"),
        P("fsdp", None),
        P("fsdp", None),
        P("fsdp", None),
        P("fsdp", None),
        P(),
        P("fsdp"),
        P("fsdp", None),
        P("fsdp", None),
        P("fsdp", None),
    )
    axis_sizes = tuple((name, mesh.shape[name]) for name in ("seq", "fsdp"))

    def body(*arrays):
        return on_device(*arrays, axis_sizes=axis_sizes)

    return jax.shard_map(
        body,
        mesh=mesh,
        in_specs=placed,
        out_specs=(
            P("fsdp", "seq", None),
            P("fsdp", "seq", None),
            P("fsdp"),
            P("fsdp", None),
            P("fsdp", None),
            P("fsdp", None),
            P("fsdp", None),
            P(),
            P("fsdp"),
            P("fsdp", None),
            P("fsdp", None),
            P("fsdp", None),
            P(),
        ),
        check_vma=False,
    )
```

time: 2660 us -> 830 us (0.31)
  waiting for transfers between devices: 1720 us -> 397 us
  local copies, waits for them, and re-layouts: 324 us -> 67.9 us
  matrix products: 389 us -> 134 us
  Pallas kernels: 0 us -> 79.3 us
  blocking collectives: 66.4 us -> 9.67 us
  starting transfers between devices: 33.8 us -> 65.1 us
  other arithmetic: 77.1 us -> 49.5 us
    unnamed x10 -> x7, waiting for transfers between devices: 919 us -> 0.11 us
    all_gather x7 -> x3, waiting for transfers between devices: 599 us -> 25.1 us  [the longest x1 25.1 us: on_device(): attn_weight = lax.all_gather(attn_own, 'fsdp', axis=0, tiled=True)]
    ppermute x0 -> x53, waiting for transfers between devices: none -> 259 us  [the longest x48 253 us: swap(): lax.ppermute(value, 'seq', [(rank, rank ^ distance) for rank in range(4)])]
    dot_general x52 -> x10, matrix products: 326 us -> 92.4 us  [the longest x4 35.8 us: matmul_nt(): lax.dot_general(left, right, (((1,), (1,)), ((), ())), preferred_element_...]
    psum x1 -> x0, waiting for transfers between devices: 163 us -> none  [on_device(): lax.psum(summed_rows.astype(jnp.bfloat16), 'seq').astype(jnp.float32)]
    reduce_scatter x0 -> x4, waiting for transfers between devices: none -> 112 us  [over_shards(): return lax.psum_scatter(gradient, 'fsdp', scatter_dimension=0, tiled=True)]
    another operation x11 -> x5, local copies, waits for them, and re-layouts: 84.1 us -> 3.41 us  [the longest x1 3.23 us: on_device(): jnp.stack([live_sum(x_in), live_sum(attn_out), live_sum(middle), live_sum...]
    pallas_call x0 -> x8, Pallas kernels: none -> 79.3 us  [the longest x1 28.3 us: attention_backward(): pl.pallas_call(body, out_shape=[jax.ShapeDtypeStruct(qkv.shape, bf16), ja...]
  transfers between devices with their start and end apart: 17 -> 60, of which waited for: 12 -> 35; matrix products, arithmetic and copies ran while one was open for 12% -> 24% of each run, Pallas kernels for 0% -> 9%
where the time goes in v1:
time: 830 us; the launch traced here: 818 us
  waiting for transfers between devices  397 us (48%)
  matrix products  134 us (16%)
  Pallas kernels  79.3 us (10%)
  local copies, waits for them, and re-layouts  67.9 us (8%)
  starting transfers between devices  65.1 us (8%)
  other arithmetic  49.5 us (6%)
  between operations  15.8 us (2%)
  blocking collectives  9.67 us (1%)
    ppermute x48, waiting for transfers between devices, swap(): lax.ppermute(value, 'seq', [(rank, rank ^ distance) for rank in range(4)])  253 us
    reduce_scatter x4, waiting for transfers between devices, over_shards(): return lax.psum_scatter(gradient, 'fsdp', scatter_dimension=0, tiled=True)  112 us
    ppermute x48, starting transfers between devices, swap(): lax.ppermute(value, 'seq', [(rank, rank ^ distance) for rank in range(4)])  57.1 us
    dot_general x4, matrix products, trans_dot(): lax.dot_general(left_side, right_side, (((0,), (0,)), ((), ())), preferre...  42.1 us
    dot_general x4, matrix products, matmul_nt(): lax.dot_general(left, right, (((1,), (1,)), ((), ())), preferred_element_...  35.8 us
    pallas_call x1, Pallas kernels, attention_backward(): pl.pallas_call(body, out_shape=[jax.ShapeDtypeStruct(qkv.shape, bf16), ja...  28.3 us
    pallas_call x1, Pallas kernels, attention_forward(): pl.pallas_call(body, out_shape=[jax.ShapeDtypeStruct((length, pairs * LAN...  26.6 us
    all_gather x1, waiting for transfers between devices, on_device(): attn_weight = lax.all_gather(attn_own, 'fsdp', axis=0, tiled=True)  25.1 us
  transfers between devices with their start and end apart: 60, of which 35 were waited for; matrix products, arithmetic and copies ran while one was open for 24% of the time, Pallas kernels for 9%

profile of v1, /device:TPU:8, one launch (start us, length us, event | category | flops | bytes accessed | tf_op | source)
XLA Modules:
  0.0 818.4 jit_solution(3604808539717928418)
XLA Ops:
  17.9 8.5 %copy.44 = pred[384,128,32]{1,2,0:T(32,128)(4,1)S(1)} copy(pred[384,128,32]{0,2,1:T(32,128)(4,1)S(1)} %iota_compare_fusion) | data formatting | bytes 3145728 | tf_op jit(solution)/shard_map/eq | solution.py:36
  26.5 9.7 %all_gather.12 = bf16[2,2048]{1,0:T(2,128)(2,1)S(1)} all-gather(bf16[2,256]{1,0:T(2,128)(2,1)S(1)} %pad_maximum_fusion.13), channel_id=1, replica_groups=mesh['seq'=4,'fsdp'=8] {'fsdp'}, dimensions={1}, use_global_device_ids=true | all-gather | bytes 9216 | tf_op jit(solution)/shard_map/all_gather | solution.py:485
  65.7 25.1 %all-gather.4.cloned.1.call-done = bf16[2048,2048]{1,0:T(8,128)(2,1)} async-done(((bf16[256,2048]{1,0:T(8,128)(2,1)}), bf16[2048,2048]{1,0:T(8,128)(2,1)}) %all-gather.4.cloned.1.call-update) | async-done | bytes 8388624 | tf_op jit(solution)/shard_map/all_gather | solution.py:479
  90.8 11.4 %fusion.15.refs_2_ = bf16[1024,1536]{1,0:T(8,128)(2,1)} fusion(bf16[2048,2048]{1,0:T(8,128)(2,1)} %all-gather.4.cloned.1.call-done, bf16[1024,2048]{1,0:T(8,128)(2,1)} %constant_dynamic-update-slice_fusion, f32[2048]{0:T(1024)S(1)} %bitcast.98, f32[1024]{0:T(1024)S(1)} %add_rsqrt_fusion), kind=kOutput, calls=%fused_computation.30 | convolution fusion | flops 6452412416 | bytes 13643776 | tf_op jit(solution)/shard_map/dot_general | solution.py:507
  103.3 26.6 %attention_forward.1 = (bf16[1024,512]{1,0:T(8,128)(2,1)}, f32[4,8,256]{2,1,0:T(8,128)}) custom-call(s32[1]{0:T(128)} %bitcast.rank_ref.refs_0_, s32[1024]{0:T(1024)} %bitcast.102, bf16[1024,1536]{1,0:T(8,128)(2,1)} %fusion.15.refs_2_, f32[4,384,256]{2,1,0:T(8,128)} %reshape.392.refs_3_.refs_6_, f32[4,8,256]{2,1,0:T(8,128)} %pad.16.refs_4_.refs_7_, ...), custom_call_target="tpu_custom_call" | custom-call | tf_op jit(solution)/shard_map/attention_forward/pallas_call | solution.py:352
  139.8 22.1 %collective-permute-done.4 = bf16[256,2048]{1,0:T(8,128)(2,1)} collective-permute-done((bf16[256,2048]{1,0:T(8,128)(2,1)S(1)}, bf16[256,2048]{1,0:T(8,128)(2,1)}, u32[]{:S(2)}, u32[]{:S(2)}) %collective-permute-start.4) | collective-permute-done | bytes 1048608 | tf_op jit(solution)/shard_map/ppermute | solution.py:40
  166.4 10.1 %collective-permute-done.5 = bf16[128,2048]{1,0:T(8,128)(2,1)S(1)} collective-permute-done((bf16[128,2048]{1,0:T(8,128)(2,1)S(1)}, bf16[128,2048]{1,0:T(8,128)(2,1)S(1)}, u32[]{:S(2)}, u32[]{:S(2)}) %collective-permute-start.5) | collective-permute-done | bytes 524320 | tf_op jit(solution)/shard_map/ppermute | solution.py:40
  181.4 9.7 %collective-permute-done.16 = bf16[256,2048]{1,0:T(8,128)(2,1)S(1)} collective-permute-done((bf16[256,2048]{1,0:T(8,128)(2,1)}, bf16[256,2048]{1,0:T(8,128)(2,1)S(1)}, u32[]{:S(2)}, u32[]{:S(2)}) %collective-permute-start.16) | collective-permute-done | bytes 1048608 | tf_op jit(solution)/shard_map/ppermute | solution.py:40
  191.7 8.8 %collective-permute-done.7 = bf16[128,2048]{1,0:T(8,128)(2,1)S(1)} collective-permute-done((bf16[128,2048]{1,0:T(8,128)(2,1)S(1)}, bf16[128,2048]{1,0:T(8,128)(2,1)S(1)}, u32[]{:S(2)}, u32[]{:S(2)}) %collective-permute-start.7) | collective-permute-done | bytes 524320 | tf_op jit(solution)/shard_map/ppermute | solution.py:40
  207.5 10.0 %collective-permute-done.18 = bf16[128,2048]{1,0:T(8,128)(2,1)S(1)} collective-permute-done((bf16[128,2048]{1,0:T(8,128)(2,1)S(1)}, bf16[128,2048]{1,0:T(8,128)(2,1)S(1)}, u32[]{:S(2)}, u32[]{:S(2)}) %collective-permute-start.18) | collective-permute-done | bytes 524320 | tf_op jit(solution)/shard_map/ppermute | solution.py:40
  217.5 12.1 %collective-permute-done.8 = bf16[256,2048]{1,0:T(8,128)(2,1)S(1)} collective-permute-done((bf16[256,2048]{1,0:T(8,128)(2,1)S(1)}, bf16[256,2048]{1,0:T(8,128)(2,1)S(1)}, u32[]{:S(2)}, u32[]{:S(2)}) %collective-permute-start.8) | collective-permute-done | bytes 1048608 | tf_op jit(solution)/shard_map/ppermute | solution.py:40
  230.0 8.0 collective-permute-done.19
  250.3 17.7 %fusion.65 = f32[1024,2560]{1,0:T(8,128)} fusion(bf16[1024,2048]{1,0:T(8,128)(2,1)} %constant_dynamic-update-slice_fusion.5, bf16[2048,2560]{1,0:T(8,128)(2,1)} %all-gather.6.cloned.1.call-done), kind=kOutput, calls=%fused_computation.168 | convolution fusion | flops 10737418240 | bytes 25165824 | tf_op jit(solution)/shard_map/dot_general | solution.py:514
  268.0 16.0 %fusion.14 = (bf16[1024,1280]{1,0:T(8,128)(2,1)S(1)}, bf16[1024,1280]{1,0:T(8,128)(2,1)S(1)}, bf16[1024,1280]{1,0:T(8,128)(2,1)}) fusion(f32[1024,2560]{1,0:T(8,128)} %fusion.65, bf16[1024,2048]{1,0:T(8,128)(2,1)} %copy-done.23, bf16[2048,1280]{1,0:T(8,128)(2,1)} %all-gather.8.cloned.1.call-done), kind=kOutput, calls=%fused_computation.22 | convolution fusion | flops 5401477120 | bytes 27787264 | tf_op jit(solution)/shard_map/dot_general | solution.py:523
  285.5 13.9 %convolution_convert_fusion.3 = bf16[1024,2048]{1,0:T(8,128)(2,1)S(1)} fusion(bf16[2048,2560]{1,0:T(8,128)(2,1)} %all-gather.6.cloned.1.call-done, bf16[1024,1280]{1,0:T(8,128)(2,1)S(1)} %get-tuple-element.73, bf16[1024,1280]{1,0:T(8,128)(2,1)S(1)} %get-tuple-element.72), kind=kOutput, calls=%fused_computation.29 | convolution fusion | flops 10750001152 | bytes 19922944 | tf_op jit(solution)/shard_map/dot_general | solution.py:157
  302.0 7.7 convolution_convert_fusion.4
  312.4 13.6 %collective-permute-done.20 = bf16[256,2048]{1,0:T(8,128)(2,1)S(1)} collective-permute-done((bf16[256,2048]{1,0:T(8,128)(2,1)S(1)}, bf16[256,2048]{1,0:T(8,128)(2,1)S(1)}, u32[]{:S(2)}, u32[]{:S(2)}) %collective-permute-start.20) | collective-permute-done | bytes 1048608 | tf_op jit(solution)/shard_map/ppermute | solution.py:40
  328.4 16.7 %collective-permute-done.12 = bf16[256,2048]{1,0:T(8,128)(2,1)S(1)} collective-permute-done((bf16[256,2048]{1,0:T(8,128)(2,1)S(1)}, bf16[256,2048]{1,0:T(8,128)(2,1)S(1)}, u32[]{:S(2)}, u32[]{:S(2)}) %collective-permute-start.12) | collective-permute-done | bytes 1048608 | tf_op jit(solution)/shard_map/ppermute | solution.py:40
  350.1 21.4 %collective-permute-done.14 = bf16[256,2048]{1,0:T(8,128)(2,1)S(1)} collective-permute-done((bf16[256,2048]{1,0:T(8,128)(2,1)S(1)}, bf16[256,2048]{1,0:T(8,128)(2,1)S(1)}, u32[]{:S(2)}, u32[]{:S(2)}) %collective-permute-start.14) | collective-permute-done | bytes 1048608 | tf_op jit(solution)/shard_map/ppermute | solution.py:40
  381.2 7.5 collective-permute-done.15
  397.9 18.4 %collective-permute-done.24 = bf16[256,2048]{1,0:T(8,128)(2,1)S(1)} collective-permute-done((bf16[256,2048]{1,0:T(8,128)(2,1)S(1)}, bf16[256,2048]{1,0:T(8,128)(2,1)S(1)}, u32[]{:S(2)}, u32[]{:S(2)}) %collective-permute-start.24) | collective-permute-done | bytes 1048608 | tf_op jit(solution)/shard_map/ppermute | solution.py:40
  421.3 6.6 collective-permute-done.26
  435.9 9.8 %convolution_convert_fusion.1 = bf16[2048,1280]{1,0:T(8,128)(2,1)} fusion(bf16[1024,2048]{1,0:T(8,128)(2,1)} %copy-done.23, bf16[1024,1280]{1,0:T(8,128)(2,1)} %get-tuple-element.74), kind=kOutput, calls=%fused_computation.8 | convolution fusion | flops 5371330560 | bytes 12058624 | tf_op jit(solution)/shard_map/dot_general | solution.py:496
  452.4 28.3 %attention_backward.1 = (bf16[1024,1536]{1,0:T(8,128)(2,1)}, f32[4,384,256]{2,1,0:T(8,128)}, f32[4,8,256]{2,1,0:T(8,128)}) custom-call(s32[1]{0:T(128)} %bitcast.rank_ref.refs_0_, s32[1024]{0:T(1024)} %bitcast.103, bf16[1024,1536]{1,0:T(8,128)(2,1)} %fusion.15.refs_2_, bf16[1024,512]{1,0:T(8,128)(2,1)} %get-tuple-element.49.refs_3_, ...), custom_call_target="tpu_custom_call" | custom-call | tf_op jit(solution)/shard_map/attention_backward/pallas_call | solution.py:385
  480.7 11.5 %convolution_convert_fusion.2 = bf16[2048,1536]{1,0:T(8,128)(2,1)} fusion(bf16[1024,1536]{1,0:T(8,128)(2,1)} %get-tuple-element.53, bf16[1024,2048]{1,0:T(8,128)(2,1)} %constant_dynamic-update-slice_fusion, f32[2048]{0:T(1024)S(1)} %bitcast.99, f32[1024]{0:T(1024)S(1)} %add_rsqrt_fusion), kind=kOutput, calls=%fused_computation.9 | convolution fusion | flops 6453985280 | bytes 13643776 | tf_op jit(solution)/shard_map/dot_general | solution.py:496
  492.3 17.0 %convolution_convert_fusion = bf16[2048,2560]{1,0:T(8,128)(2,1)} fusion(bf16[1024,2048]{1,0:T(8,128)(2,1)} %constant_dynamic-update-slice_fusion.5, bf16[1024,1280]{1,0:T(8,128)(2,1)} %copy-done.39, bf16[1024,1280]{1,0:T(8,128)(2,1)} %copy-done.38), kind=kOutput, calls=%fused_computation | convolution fusion | flops 10753146880 | bytes 19922944 | tf_op jit(solution)/shard_map/dot_general | solution.py:496
  509.3 9.8 %fusion.18 = bf16[1024,2048]{1,0:T(8,128)(2,1)S(1)} fusion(bf16[1024,1536]{1,0:T(8,128)(2,1)} %get-tuple-element.53, bf16[2048,2048]{1,0:T(8,128)(2,1)} %all-gather.4.cloned.1.call-done), kind=kOutput, calls=%fused_computation.31 | convolution fusion | flops 6444548096 | bytes 13631488 | tf_op jit(solution)/shard_map/dot_general | solution.py:157
  551.3 13.5 %collective-permute-done.30 = bf16[256,2048]{1,0:T(8,128)(2,1)} collective-permute-done((bf16[256,2048]{1,0:T(8,128)(2,1)}, bf16[256,2048]{1,0:T(8,128)(2,1)}, u32[]{:S(2)}, u32[]{:S(2)}) %collective-permute-start.30) | collective-permute-done | bytes 1048608 | tf_op jit(solution)/shard_map/ppermute | solution.py:40
  605.8 106.0 %reduce-scatter.9.cloned.1.call-done.own_ref = bf16[256,2560]{1,0:T(8,128)(2,1)} async-done(((bf16[2048,2560]{1,0:T(8,128)(2,1)}), bf16[256,2560]{1,0:T(8,128)(2,1)}) %reduce-scatter.9.cloned.1.call-update) | async-done | bytes 1310736 | tf_op jit(solution)/shard_map/reduce_scatter | solution.py:501
  728.0 27.0 %collective-permute-done.38.lo_ref = bf16[128,512]{1,0:T(8,128)(2,1)S(1)} collective-permute-done((bf16[128,512]{1,0:T(8,128)(2,1)S(1)}, bf16[128,512]{1,0:T(8,128)(2,1)S(1)}, u32[]{:S(2)}, u32[]{:S(2)}) %collective-permute-start.38) | collective-permute-done | bytes 131104 | tf_op jit(solution)/shard_map/ppermute | solution.py:40
  786.1 9.6 %collective-permute-done.47.lo_ref = bf16[128,2560]{1,0:T(8,128)(2,1)S(1)} collective-permute-done((bf16[128,2560]{1,0:T(8,128)(2,1)S(1)}, bf16[128,2560]{1,0:T(8,128)(2,1)S(1)}, u32[]{:S(2)}, u32[]{:S(2)}) %collective-permute-start.47) | collective-permute-done | bytes 655392 | tf_op jit(solution)/shard_map/ppermute | solution.py:40
  798.2 6.6 column_place.6
  (324 shorter events, 262.0 us)
Async XLA Ops:
  7.2 83.6 %all-gather.4.cloned.1.call-start = ((), (), s32[]{:S(2)}) async-start(), calls=%async_computation.4 | async-start | bytes 9437184 | tf_op jit(solution)/shard_map/all_gather | solution.py:479
  9.7 240.6 %all-gather.6.cloned.1.call-start = ((), (), s32[]{:S(2)}) async-start(), calls=%async_computation.5 | async-start | bytes 11796480 | tf_op jit(solution)/shard_map/all_gather | solution.py:483
  12.7 255.3 %all-gather.8.cloned.1.call-start = ((), (), s32[]{:S(2)}) async-start(), calls=%async_computation.6 | async-start | bytes 5898240 | tf_op jit(solution)/shard_map/all_gather | solution.py:484
  12.8 25.9 %collective-permute-start = (bf16[256,2048]{1,0:T(8,128)(2,1)S(1)}, bf16[256,2048]{1,0:T(8,128)(2,1)}, u32[]{:S(2)}, u32[]{:S(2)}) collective-permute-start(bf16[256,2048]{1,0:T(8,128)(2,1)S(1)} %bitcast.80), channel_id=1, source_target_pairs={{0,8},{8,0},{16,24},{24,16},{1,9},{9,1},{17,25},{25,17},{2,10},{10... | collective-permute-start | bytes 3145736 | tf_op jit(solution)/shard_map/ppermute | solution.py:40
  14.3 32.6 %collective-permute-start.1 = (bf16[256,2048]{1,0:T(8,128)(2,1)S(1)}, bf16[256,2048]{1,0:T(8,128)(2,1)}, u32[]{:S(2)}, u32[]{:S(2)}) collective-permute-start(bf16[256,2048]{1,0:T(8,128)(2,1)S(1)} %bitcast.81), channel_id=1, source_target_pairs={{0,16},{8,24},{16,0},{24,8},{1,17},{9,25},{17,1},{25,9},{2,18},{10... | collective-permute-start | bytes 3145736 | tf_op jit(solution)/shard_map/ppermute | solution.py:40
  138.1 448.8 %reduce-scatter.7.cloned.1.call-start = ((), (), s32[]{:S(2)}) async-start(), calls=%async_computation.8 | async-start | bytes 2359296 | tf_op jit(solution)/shard_map/reduce_scatter | solution.py:501
  138.3 28.1 %collective-permute-start.6 = (bf16[256,2048]{1,0:T(8,128)(2,1)S(1)}, bf16[256,2048]{1,0:T(8,128)(2,1)S(1)}, u32[]{:S(2)}, u32[]{:S(2)}) collective-permute-start(bf16[256,2048]{1,0:T(8,128)(2,1)S(1)} %pad_maximum_fusion.5), channel_id=1, source_target_pairs={{0,16},{8,24},{16,0},{24,8},{1,17},{9,25},{17,1},{25,9},{2,18},{10... | collective-permute-start | bytes 3145736 | tf_op jit(solution)/shard_map/ppermute | solution.py:40
  164.9 26.2 %collective-permute-start.16 = (bf16[256,2048]{1,0:T(8,128)(2,1)}, bf16[256,2048]{1,0:T(8,128)(2,1)S(1)}, u32[]{:S(2)}, u32[]{:S(2)}) collective-permute-start(bf16[256,2048]{1,0:T(8,128)(2,1)} %bitcast.14), channel_id=1, source_target_pairs={{0,8},{8,0},{16,24},{24,16},{1,9},{9,1},{17,25},{25,17},{2,10},{10... | collective-permute-start | bytes 3145736 | tf_op jit(solution)/shard_map/ppermute | solution.py:40
  180.0 26.8 %collective-permute-start.17 = (bf16[256,2048]{1,0:T(8,128)(2,1)}, bf16[256,2048]{1,0:T(8,128)(2,1)S(1)}, u32[]{:S(2)}, u32[]{:S(2)}) collective-permute-start(bf16[256,2048]{1,0:T(8,128)(2,1)} %bitcast.14), channel_id=1, source_target_pairs={{0,16},{8,24},{16,0},{24,8},{1,17},{9,25},{17,1},{25,9},{2,18},{10... | collective-permute-start | bytes 3145736 | tf_op jit(solution)/shard_map/ppermute | solution.py:40
  191.2 26.3 %collective-permute-start.18 = (bf16[128,2048]{1,0:T(8,128)(2,1)S(1)}, bf16[128,2048]{1,0:T(8,128)(2,1)S(1)}, u32[]{:S(2)}, u32[]{:S(2)}) collective-permute-start(bf16[128,2048]{1,0:T(8,128)(2,1)S(1)} %slice.383), channel_id=1, source_target_pairs={{0,16},{8,24},{16,0},{24,8},{1,17},{9,25},{17,1},{25,9},{2,18},{10... | collective-permute-start | bytes 1572872 | tf_op jit(solution)/shard_map/ppermute | solution.py:40
  203.5 26.0 %collective-permute-start.8 = (bf16[256,2048]{1,0:T(8,128)(2,1)S(1)}, bf16[256,2048]{1,0:T(8,128)(2,1)S(1)}, u32[]{:S(2)}, u32[]{:S(2)}) collective-permute-start(bf16[256,2048]{1,0:T(8,128)(2,1)S(1)} %get-tuple-element.71), channel_id=1, source_target_pairs={{0,8},{8,0},{16,24},{24,16},{1,9},{9,1},{17,25},{25,17},{2,10},{10... | collective-permute-start | bytes 3145736 | tf_op jit(solution)/shard_map/ppermute | solution.py:40
  205.0 35.0 %collective-permute-start.9 = (bf16[256,2048]{1,0:T(8,128)(2,1)S(1)}, bf16[256,2048]{1,0:T(8,128)(2,1)S(1)}, u32[]{:S(2)}, u32[]{:S(2)}) collective-permute-start(bf16[256,2048]{1,0:T(8,128)(2,1)S(1)} %get-tuple-element.71), channel_id=1, source_target_pairs={{0,16},{8,24},{16,0},{24,8},{1,17},{9,25},{17,1},{25,9},{2,18},{10... | collective-permute-start | bytes 3145736 | tf_op jit(solution)/shard_map/ppermute | solution.py:40
  206.8 31.2 %collective-permute-start.19 = (bf16[128,2048]{1,0:T(8,128)(2,1)S(1)}, bf16[128,2048]{1,0:T(8,128)(2,1)S(1)}, u32[]{:S(2)}, u32[]{:S(2)}) collective-permute-start(bf16[128,2048]{1,0:T(8,128)(2,1)S(1)} %slice.384), channel_id=1, source_target_pairs={{0,8},{8,0},{16,24},{24,16},{1,9},{9,1},{17,25},{25,17},{2,10},{10... | collective-permute-start | bytes 1572872 | tf_op jit(solution)/shard_map/ppermute | solution.py:40
  299.9 26.1 %collective-permute-start.20 = (bf16[256,2048]{1,0:T(8,128)(2,1)S(1)}, bf16[256,2048]{1,0:T(8,128)(2,1)S(1)}, u32[]{:S(2)}, u32[]{:S(2)}) collective-permute-start(bf16[256,2048]{1,0:T(8,128)(2,1)S(1)} %pad_maximum_fusion.8), channel_id=1, source_target_pairs={{0,8},{8,0},{16,24},{24,16},{1,9},{9,1},{17,25},{25,17},{2,10},{10... | collective-permute-start | bytes 3145736 | tf_op jit(solution)/shard_map/ppermute | solution.py:40
  310.1 34.9 %collective-permute-start.12 = (bf16[256,2048]{1,0:T(8,128)(2,1)S(1)}, bf16[256,2048]{1,0:T(8,128)(2,1)S(1)}, u32[]{:S(2)}, u32[]{:S(2)}) collective-permute-start(bf16[256,2048]{1,0:T(8,128)(2,1)S(1)} %pad_maximum_fusion.6), channel_id=1, source_target_pairs={{0,8},{8,0},{16,24},{24,16},{1,9},{9,1},{17,25},{25,17},{2,10},{10... | collective-permute-start | bytes 3145736 | tf_op jit(solution)/shard_map/ppermute | solution.py:40
  311.7 35.0 %collective-permute-start.22 = (bf16[256,2048]{1,0:T(8,128)(2,1)S(1)}, bf16[256,2048]{1,0:T(8,128)(2,1)S(1)}, u32[]{:S(2)}, u32[]{:S(2)}) collective-permute-start(bf16[256,2048]{1,0:T(8,128)(2,1)S(1)} %pad_maximum_fusion.9), channel_id=1, source_target_pairs={{0,16},{8,24},{16,0},{24,8},{1,17},{9,25},{17,1},{25,9},{2,18},{10... | collective-permute-start | bytes 3145736 | tf_op jit(solution)/shard_map/ppermute | solution.py:40
  327.6 43.9 %collective-permute-start.14 = (bf16[256,2048]{1,0:T(8,128)(2,1)S(1)}, bf16[256,2048]{1,0:T(8,128)(2,1)S(1)}, u32[]{:S(2)}, u32[]{:S(2)}) collective-permute-start(bf16[256,2048]{1,0:T(8,128)(2,1)S(1)} %pad_maximum_fusion.7), channel_id=1, source_target_pairs={{0,16},{8,24},{16,0},{24,8},{1,17},{9,25},{17,1},{25,9},{2,18},{10... | collective-permute-start | bytes 3145736 | tf_op jit(solution)/shard_map/ppermute | solution.py:40
  345.1 32.8 %collective-permute-start.13 = (bf16[128,2048]{1,0:T(8,128)(2,1)S(1)}, bf16[128,2048]{1,0:T(8,128)(2,1)S(1)}, u32[]{:S(2)}, u32[]{:S(2)}) collective-permute-start(bf16[128,2048]{1,0:T(8,128)(2,1)S(1)} %add_convert_fusion.5), channel_id=1, source_target_pairs={{0,16},{8,24},{16,0},{24,8},{1,17},{9,25},{17,1},{25,9},{2,18},{10... | collective-permute-start | bytes 1572872 | tf_op jit(solution)/shard_map/ppermute | solution.py:40
  349.5 30.7 %collective-permute-start.23 = (bf16[128,2048]{1,0:T(8,128)(2,1)S(1)}, bf16[128,2048]{1,0:T(8,128)(2,1)S(1)}, u32[]{:S(2)}, u32[]{:S(2)}) collective-permute-start(bf16[128,2048]{1,0:T(8,128)(2,1)S(1)} %get-tuple-element.82), channel_id=1, source_target_pairs={{0,8},{8,0},{16,24},{24,16},{1,9},{9,1},{17,25},{25,17},{2,10},{10... | collective-permute-start | bytes 1572872 | tf_op jit(solution)/shard_map/ppermute | solution.py:40
  435.9 152.6 %reduce-scatter.11.cloned.1.call-start = ((), (), s32[]{:S(2)}) async-start(), calls=%async_computation.10 | async-start | bytes 5898240 | tf_op jit(solution)/shard_map/reduce_scatter | solution.py:501
  445.7 156.0 %reduce-scatter.5.cloned.1.call-start = ((), (), s32[]{:S(2)}) async-start(), calls=%async_computation.7 | async-start | bytes 7077888 | tf_op jit(solution)/shard_map/reduce_scatter | solution.py:501
  492.2 219.7 %reduce-scatter.9.cloned.1.call-start = ((), (), s32[]{:S(2)}) async-start(), calls=%async_computation.9 | async-start | bytes 11796480 | tf_op jit(solution)/shard_map/reduce_scatter | solution.py:501
  549.5 26.1 %collective-permute-start.40 = (f32[33,32]{1,0:T(8,128)S(1)}, f32[33,32]{1,0:T(8,128)S(1)}, u32[]{:S(2)}, u32[]{:S(2)}) collective-permute-start(f32[33,32]{1,0:T(8,128)S(1)} %pad_maximum_fusion.12), channel_id=1, source_target_pairs={{0,8},{8,0},{16,24},{24,16},{1,9},{9,1},{17,25},{25,17},{2,10},{10... | collective-permute-start | bytes 12680 | tf_op jit(solution)/shard_map/ppermute | solution.py:75
  588.5 124.9 %collective-permute-start.49 = (bf16[256,1280]{1,0:T(8,128)(2,1)}, bf16[256,1280]{1,0:T(8,128)(2,1)}, u32[]{:S(2)}, u32[]{:S(2)}) collective-permute-start(bf16[256,1280]{1,0:T(8,128)(2,1)} %reduce-scatter.11.cloned.1.call-done.own_ref), channel_id=1, source_target_pairs={{0,8},{8,0},{16,24},{24,16},{1,9},{9,1},{17,25},{25,17},{2,10},{10... | collective-permute-start | bytes 1966088 | tf_op jit(solution)/shard_map/ppermute | solution.py:40
  594.8 122.6 %collective-permute-start.50 = (bf16[256,1280]{1,0:T(8,128)(2,1)}, bf16[256,1280]{1,0:T(8,128)(2,1)}, u32[]{:S(2)}, u32[]{:S(2)}) collective-permute-start(bf16[256,1280]{1,0:T(8,128)(2,1)} %reduce-scatter.11.cloned.1.call-done.own_ref), channel_id=1, source_target_pairs={{0,16},{8,24},{16,0},{24,8},{1,17},{9,25},{17,1},{25,9},{2,18},{10... | collective-permute-start | bytes 1966088 | tf_op jit(solution)/shard_map/ppermute | solution.py:40
  601.8 118.9 %collective-permute-start.32 = (bf16[256,1536]{1,0:T(8,128)(2,1)}, bf16[256,1536]{1,0:T(8,128)(2,1)}, u32[]{:S(2)}, u32[]{:S(2)}) collective-permute-start(bf16[256,1536]{1,0:T(8,128)(2,1)} %reduce-scatter.5.cloned.1.call-done.own_ref), channel_id=1, source_target_pairs={{0,8},{8,0},{16,24},{24,16},{1,9},{9,1},{17,25},{25,17},{2,10},{10... | collective-permute-start | bytes 2359304 | tf_op jit(solution)/shard_map/ppermute | solution.py:40
  603.2 118.9 %collective-permute-start.33 = (bf16[256,1536]{1,0:T(8,128)(2,1)}, bf16[256,1536]{1,0:T(8,128)(2,1)}, u32[]{:S(2)}, u32[]{:S(2)}) collective-permute-start(bf16[256,1536]{1,0:T(8,128)(2,1)} %reduce-scatter.5.cloned.1.call-done.own_ref), channel_id=1, source_target_pairs={{0,16},{8,24},{16,0},{24,8},{1,17},{9,25},{17,1},{25,9},{2,18},{10... | collective-permute-start | bytes 2359304 | tf_op jit(solution)/shard_map/ppermute | solution.py:40
  711.9 66.5 %collective-permute-start.45 = (bf16[256,2560]{1,0:T(8,128)(2,1)}, bf16[256,2560]{1,0:T(8,128)(2,1)}, u32[]{:S(2)}, u32[]{:S(2)}) collective-permute-start(bf16[256,2560]{1,0:T(8,128)(2,1)} %reduce-scatter.9.cloned.1.call-done.own_ref), channel_id=1, source_target_pairs={{0,8},{8,0},{16,24},{24,16},{1,9},{9,1},{17,25},{25,17},{2,10},{10... | collective-permute-start | bytes 3932168 | tf_op jit(solution)/shard_map/ppermute | solution.py:40
  713.4 67.8 %collective-permute-start.46 = (bf16[256,2560]{1,0:T(8,128)(2,1)}, bf16[256,2560]{1,0:T(8,128)(2,1)}, u32[]{:S(2)}, u32[]{:S(2)}) collective-permute-start(bf16[256,2560]{1,0:T(8,128)(2,1)} %reduce-scatter.9.cloned.1.call-done.own_ref), channel_id=1, source_target_pairs={{0,16},{8,24},{16,0},{24,8},{1,17},{9,25},{17,1},{25,9},{2,18},{10... | collective-permute-start | bytes 3932168 | tf_op jit(solution)/shard_map/ppermute | solution.py:40
  717.4 39.5 %collective-permute-start.51 = (bf16[128,1280]{1,0:T(8,128)(2,1)S(1)}, bf16[128,1280]{1,0:T(8,128)(2,1)}, u32[]{:S(2)}, u32[]{:S(2)}) collective-permute-start(bf16[128,1280]{1,0:T(8,128)(2,1)S(1)} %slice.420), channel_id=1, source_target_pairs={{0,16},{8,24},{16,0},{24,8},{1,17},{9,25},{17,1},{25,9},{2,18},{10... | collective-permute-start | bytes 983048 | tf_op jit(solution)/shard_map/ppermute | solution.py:40
  720.6 34.3 %collective-permute-start.38 = (bf16[128,512]{1,0:T(8,128)(2,1)S(1)}, bf16[128,512]{1,0:T(8,128)(2,1)S(1)}, u32[]{:S(2)}, u32[]{:S(2)}) collective-permute-start(bf16[128,512]{1,0:T(8,128)(2,1)S(1)} %slice.413), channel_id=1, source_target_pairs={{0,16},{8,24},{16,0},{24,8},{1,17},{9,25},{17,1},{25,9},{2,18},{10... | collective-permute-start | bytes 393224 | tf_op jit(solution)/shard_map/ppermute | solution.py:40
  722.2 33.3 %collective-permute-start.39 = (bf16[128,512]{1,0:T(8,128)(2,1)S(1)}, bf16[128,512]{1,0:T(8,128)(2,1)S(1)}, u32[]{:S(2)}, u32[]{:S(2)}) collective-permute-start(bf16[128,512]{1,0:T(8,128)(2,1)S(1)} %slice.414), channel_id=1, source_target_pairs={{0,8},{8,0},{16,24},{24,16},{1,9},{9,1},{17,25},{25,17},{2,10},{10... | collective-permute-start | bytes 393224 | tf_op jit(solution)/shard_map/ppermute | solution.py:40
  (68 other events, 1233.0 us)
Sparse Core Ops, SparseCore 0:
  10.2 80.5 all-gather.3
  93.0 97.6 all-gather.5
  193.0 55.4 all-gather.7
  436.0 32.3 reduce-scatter.6
  471.1 59.3 reduce-scatter.10
  532.6 69.0 reduce-scatter.4
  604.1 107.7 reduce-scatter.8
